TPU v7x, 128 devices: a whole 4x4x4 slice. The times are simulated.
128 devices in a mesh: sec: 4 (over y), dp: 8 (over x_hi, z), mp: 4 (over x_lo, core).
Axes of the slice: x: 4 (x_hi: 2, x_lo: 2; x = x_hi * 2 + x_lo), y: 4, z: 4, core: 2. Of those that a mesh axis runs over, the one named last changes fastest.
Arguments:
- patches: bfloat16 [320, 5120], P('dp'), may hold values from -6 to 6
- ln_gain: bfloat16 [1280], replicated, may hold values from 0.099609375 to 1.8984375
- ln_shift: bfloat16 [1280], replicated, may hold values from -3 to 3
- w_in: bfloat16 [5120, 5120], P('dp', ('sec', 'mp')), may hold values from -0.078125 to 0.078125
- b_in: bfloat16 [5120], P(('sec', 'mp')), may hold values from -3 to 3
- w_out: bfloat16 [5120, 8192], P(('sec', 'mp'), 'dp'), may hold values from -0.125 to 0.125
- b_out: bfloat16 [8192], P(('sec', 'mp')), may hold values from -3 to 3
- place: int32 [320], P('dp'), may hold values from 0 to 255, as said below
- image_counts: int32 [8], P('dp'), may hold values from 1 to 40, 128 in all
- text_rows: bfloat16 [2048, 8192], P('dp', ('sec', 'mp')), may hold values from -6 to 6
- segments: int32 [8, 256], P('dp'), may hold values from 0 to 3, never falling along the last dimension, each value on 1 to 128 neighbouring positions
- norm_gain: bfloat16 [2, 8192], replicated, may hold values from 0.099609375 to 1.8984375
- q_weight: bfloat16 [2, 8192, 4096], P(None, None, ('sec', 'mp'))
- kv_weight: bfloat16 [2, 2, 512, 8192], P(None, None, ('sec', 'mp'))
- o_weight: bfloat16 [2, 4096, 8192], P(None, ('sec', 'mp')), may hold values from -0.125 to 0.125
- grad_rows: bfloat16 [320, 8192], P('dp'), may hold values from -6 to 6
Outputs:
- final_rows: float32 [2048, 8192], P('dp', ('sec', 'mp'))
- patch_grads: float32 [320, 5120], P('dp')
Inputs may be any that keep to these rules, and one draw needn't show every extreme that they name: `place`: each owner's 40 entries are distinct token positions of its own packed sequence; only an owner's first image_counts entries are used. `image_counts`: the counts sum to 8 * (16) over all owners.
All inputs are finite; a program needn't handle non-finite values. No bound on the sum of `image_counts` on one device may be relied on, other than what follows from the above.
Results may differ from a plain program's by a relative error of at most 0.0055.
Values may be sent and summed in bfloat16 or wider, within the bound.
A program may use at most 128 MiB of HBM per device.

v0:
```python
import math

import jax
import jax.numpy as jnp
from jax import lax
from jax.sharding import PartitionSpec as P

D = 8192
HEAD_DIM = 128


ln_eps = 1e-06
rms_eps = 1e-06
rope_base = 1000000.0


def group_norm(patch_rows, ln_gain, ln_shift):
    row_count = patch_rows.shape[0]
    grouped = patch_rows.astype(jnp.float32).reshape(row_count, -1, ln_gain.shape[0])
    center = grouped - jnp.mean(grouped, axis=-1, keepdims=True)
    spread = jnp.mean(center * center, axis=-1, keepdims=True)
    scaled = center * lax.rsqrt(spread + ln_eps) * ln_gain.astype(jnp.float32) + ln_shift.astype(
        jnp.float32
    )
    return scaled.reshape(row_count, -1)


def gelu_exact(values):
    return jax.nn.gelu(values, approximate=False)


def rotate(values, positions):
    head_depth = values.shape[-1]
    half_depth = head_depth // 2
    inv_freq = rope_base ** (-2.0 * jnp.arange(half_depth, dtype=jnp.float32) / head_depth)
    angles = positions[:, None] * inv_freq[None, :]
    cosine = jnp.cos(angles)[:, None, :]
    sine_part = jnp.sin(angles)[:, None, :]
    first_half = values[..., :half_depth]
    second = values[..., half_depth:]
    return jnp.concatenate(
        [first_half * cosine - second * sine_part, second * cosine + first_half * sine_part],
        axis=-1,
    )


def doc_mask(segment_ids):
    token_index = jnp.arange(segment_ids.shape[0], dtype=jnp.int32)
    same_doc = segment_ids[:, None] == segment_ids[None, :]
    allowed = same_doc & (token_index[None, :] <= token_index[:, None])
    positions = jnp.sum(allowed.astype(jnp.int32), axis=1) - 1
    return (allowed, positions.astype(jnp.float32))


def attend(normed, allowed, positions, q_local, kv_local):
    token_count = normed.shape[0]
    queries = jnp.dot(normed, q_local, preferred_element_type=jnp.float32).reshape(
        token_count, -1, HEAD_DIM
    )
    key_value = jnp.einsum("td,kcd->tkc", normed, kv_local, preferred_element_type=jnp.float32)
    key_value = lax.all_gather(key_value, "mp", axis=2, tiled=True)
    key_rows = rotate(key_value[:, 0:1, :], positions)[:, 0, :].astype(jnp.bfloat16)
    value_rows = key_value[:, 1, :].astype(jnp.bfloat16)
    queries = rotate(queries, positions).astype(jnp.bfloat16)
    scores = jnp.einsum("thd,sd->hts", queries, key_rows, preferred_element_type=jnp.float32) * (
        1.0 / math.sqrt(HEAD_DIM)
    )
    scores = jnp.where(allowed[None], scores, -jnp.inf)
    row_max = jnp.max(scores, axis=-1, keepdims=True)
    exp_scores = jnp.exp(scores - row_max)
    attn_weights = (exp_scores / jnp.sum(exp_scores, axis=-1, keepdims=True)).astype(jnp.bfloat16)
    attended = jnp.einsum(
        "hts,sd->thd", attn_weights, value_rows, preferred_element_type=jnp.float32
    )
    return attended.astype(jnp.bfloat16).reshape(token_count, -1)


def gather_features(rows_local):
    return lax.all_gather(rows_local, ("sec", "mp"), axis=1, tiled=True)


def section_features(rows_local, gain_row, allowed, positions, q_local, kv_local, o_local):
    share = rows_local.shape[1]
    square_sums = lax.psum(jnp.sum(rows_local * rows_local, axis=1), ("sec", "mp"))
    factor = lax.rsqrt(square_sums / D + rms_eps)
    gain_local = lax.dynamic_slice_in_dim(
        gain_row, lax.axis_index(("sec", "mp")) * share, share, 0
    ).astype(jnp.float32)
    normed_local = (rows_local * factor[:, None] * gain_local[None, :]).astype(jnp.bfloat16)
    normed = gather_features(normed_local)
    attended = attend(normed, allowed, positions, q_local, kv_local)
    summed = lax.psum_scatter(
        lax.dot_general(
            o_local, attended, (((0,), (1,)), ((), ())), preferred_element_type=jnp.float32
        ),
        ("sec", "mp"),
        scatter_dimension=0,
        tiled=True,
    )
    return rows_local + summed.T


def merger_front(patch_rows, ln_gain, ln_shift, w_in_full, b_in, w_out_full, b_out):
    normed = group_norm(patch_rows, ln_gain, ln_shift).astype(jnp.bfloat16)
    pre_act = jnp.dot(normed, w_in_full, preferred_element_type=jnp.float32) + b_in.astype(
        jnp.float32
    )
    hidden_units = gelu_exact(pre_act).astype(jnp.bfloat16)
    partial_out = jnp.dot(hidden_units, w_out_full, preferred_element_type=jnp.float32)
    merged = lax.psum_scatter(
        partial_out, ("sec", "mp"), scatter_dimension=1, tiled=True
    ) + b_out.astype(jnp.float32)
    return (merged.astype(jnp.bfloat16), pre_act)


def merger_back(patch_rows, pre_act, hidden_grads, ln_gain, ln_shift, w_in_full):
    _, pull_gelu = jax.vjp(gelu_exact, pre_act)
    pre_grads = pull_gelu(hidden_grads)[0].astype(jnp.bfloat16)
    normed_grads = lax.dot_general(
        pre_grads, w_in_full, (((1,), (1,)), ((), ())), preferred_element_type=jnp.float32
    )
    normed_grads = lax.psum(normed_grads, ("sec", "mp"))
    _, pull_norm = jax.vjp(
        lambda values: group_norm(values, ln_gain, ln_shift), patch_rows.astype(jnp.float32)
    )
    return pull_norm(normed_grads)[0]


def local(
    patches,
    ln_gain,
    ln_shift,
    w_in,
    b_in,
    w_out,
    b_out,
    place,
    image_counts,
    text_rows,
    segments,
    norm_gain,
    q_weight,
    kv_weight,
    o_weight,
    grad_rows,
):
    w_in_full, w_out_full = (
        lax.all_gather(w_in, "dp", axis=0, tiled=True),
        lax.all_gather(w_out, "dp", axis=1, tiled=True),
    )
    slot_count = patches.shape[0]
    tokens = text_rows.shape[0]
    slot_index = jnp.arange(slot_count, dtype=jnp.int32)
    live_slot = slot_index < image_counts[0]
    slot_grads = jnp.where(live_slot[:, None], grad_rows, jnp.zeros_like(grad_rows))
    hidden_grads = lax.dot_general(
        slot_grads, w_out_full, (((1,), (1,)), ((), ())), preferred_element_type=jnp.float32
    )
    merged_local, pre_act = merger_front(
        patches, ln_gain, ln_shift, w_in_full, b_in, w_out_full, b_out
    )
    patch_grads = merger_back(patches, pre_act, hidden_grads, ln_gain, ln_shift, w_in_full)
    token_index = jnp.arange(tokens, dtype=jnp.int32)
    select = (place[:, None] == token_index[None, :]) & live_slot[:, None]
    is_image = jnp.any(select, axis=0)
    picked = lax.dot_general(
        select.astype(jnp.bfloat16),
        merged_local,
        (((0,), (0,)), ((), ())),
        preferred_element_type=jnp.float32,
    )
    start_rows = jnp.where(is_image[:, None], picked, text_rows.astype(jnp.float32)).astype(
        jnp.bfloat16
    )
    allowed, positions = doc_mask(segments[0])
    layer_count = q_weight.shape[0]
    current = start_rows.astype(jnp.float32)
    for layer_index in range(layer_count):
        current = section_features(
            current,
            norm_gain[layer_index],
            allowed,
            positions,
            q_weight[layer_index],
            kv_weight[layer_index],
            o_weight[layer_index],
        )
    return (current, patch_grads)


def solution(mesh):
    in_specs = (
        P("dp", None),
        P(),
        P(),
        P("dp", ("sec", "mp")),
        P(("sec", "mp")),
        P(("sec", "mp"), "dp"),
        P(("sec", "mp")),
        P("dp"),
        P("dp"),
        P("dp", ("sec", "mp")),
        P("dp", None),
        P(),
        P(None, None, ("sec", "mp")),
        P(None, None, ("sec", "mp"), None),
        P(None, ("sec", "mp"), None),
        P("dp", None),
    )
    out_specs = (P("dp", ("sec", "mp")), P("dp", None))
    return jax.shard_map(local, mesh=mesh, in_specs=in_specs, out_specs=out_specs, check_vma=False)
```

profile of v0, /device:TPU:0, one launch (start us, length us, event | category | flops | bytes accessed | tf_op | source)
XLA Modules:
  0.0 707.5 jit_solution(7781813747117255810)
XLA Ops:
  7.2 0.7 all-gather.5.cloned.1.call-update
  8.0 0.7 all-gather.7.cloned.1.call-update
  8.7 1.4 reshape.223
  10.2 0.2 reduce_sum.78
  10.4 0.4 multiply_reduce_fusion.1
  10.7 0.2 mul.308
  10.9 0.1 copy.43
  11.1 0.2 sub.50
  11.3 0.1 copy.42
  11.5 64.8 %all-gather.5.cloned.1.call-done = bf16[5120,320]{0,1:T(8,128)(2,1)} async-done(((bf16[640,320]{0,1:T(8,128)(2,1)}), bf16[5120,320]{0,1:T(8,128)(2,1)}) %all-gather.5.cloned.1.call-update) | async-done | bytes 3276816 | tf_op jit(solution)/shard_map/all_gather | solution.py:148
  76.3 3.0 convolution_add_fusion
  79.4 77.0 %all-gather.7.cloned.1.call-done = bf16[320,8192]{1,0:T(8,128)(2,1)} async-done(((bf16[320,1024]{1,0:T(8,128)(2,1)}), bf16[320,8192]{1,0:T(8,128)(2,1)}) %all-gather.7.cloned.1.call-update) | async-done | bytes 5242896 | tf_op jit(solution)/shard_map/all_gather | solution.py:149
  156.4 4.6 fusion.88
  161.1 0.0 all-gather.9.cloned.1.call-start
  161.9 0.1 fusion.116
  161.9 0.1 fusion.87
  162.0 60.0 %reduce-scatter.4.cloned.1.call-done = f32[40,512]{1,0:T(8,128)} async-done(((f32[40,8192]{1,0:T(8,128)}), f32[40,512]{1,0:T(8,128)}) %reduce-scatter.4.cloned.1.call-update) | async-done | bytes 81936 | tf_op jit(solution)/shard_map/reduce_scatter | solution.py:110
  222.0 1.4 multiply_reduce_fusion.3
  223.4 27.7 %psum.21 = f32[256]{0:T(256)S(1)} all-reduce(f32[256]{0:T(256)S(1)} %get-tuple-element.16), channel_id=1, replica_groups=mesh['sec'=4,'dp'=8,'mp'=4] {'sec','mp'}, use_global_device_ids=true, to_apply=%region_5.6 | all-reduce | flops 256 | bytes 2048 | tf_op jit(solution)/shard_map/psum | solution.py:84
  251.1 0.8 multiply_convert_fusion.1
  252.0 0.0 reduce-scatter.6.cloned.1.call-start
  252.0 5.7 slice_bitcast_fusion.1
  257.8 6.4 copy.26
  264.2 0.1 convert_reduce_fusion
  264.3 0.1 fusion.36
  264.5 0.3 multiply_cosine_fusion
  264.8 23.3 %all-gather.9.cloned.1.call-done = bf16[256,8192]{1,0:T(8,128)(2,1)} async-done(((bf16[256,512]{1,0:T(8,128)(2,1)}), bf16[256,8192]{1,0:T(8,128)(2,1)}) %all-gather.9.cloned.1.call-update) | async-done | bytes 4194320 | tf_op jit(solution)/shard_map/all_gather | solution.py:79
  288.1 4.0 fusion.10
  292.1 5.8 all_gather.21
  297.9 0.3 fusion.52
  298.3 3.5 fusion.8
  301.8 0.6 copy-done.12
  302.4 1.0 fusion.21
  303.5 1.2 fusion.117
  304.7 1.6 convolution_convert_fusion.1
  306.3 6.7 convolution_bitcast_fusion.1
  313.1 97.8 %reduce-scatter.6.cloned.1.call-done = f32[512,256]{0,1:T(8,128)} async-done(((f32[8192,256]{0,1:T(8,128)}), f32[512,256]{0,1:T(8,128)}) %reduce-scatter.6.cloned.1.call-update) | async-done | bytes 524304 | tf_op jit(solution)/shard_map/reduce_scatter | solution.py:92
  410.9 1.2 multiply_reduce_fusion.2
  412.1 27.6 %psum.22 = f32[256]{0:T(256)S(1)} all-reduce(f32[256]{0:T(256)S(1)} %multiply_reduce_fusion.2), channel_id=1, replica_groups=mesh['sec'=4,'dp'=8,'mp'=4] {'sec','mp'}, use_global_device_ids=true, to_apply=%region_11.12 | all-reduce | flops 256 | bytes 2048 | tf_op jit(solution)/shard_map/psum | solution.py:84
  439.7 1.9 multiply_convert_fusion
  441.6 0.2 all-reduce.2.cloned.1.call-start
  441.8 6.5 copy.30
  448.3 7.6 %fusion.71 = f32[40,5120]{1,0:T(8,128)} fusion(bf16[5120,320]{0,1:T(8,128)(2,1)} %all-gather.5.cloned.1.call-done, bf16[320,8192]{1,0:T(8,128)(2,1)} %all-gather.7.cloned.1.call-done, bf16[40,8192]{1,0:T(8,128)(2,1)S(1)} %copy-done.7, pred[40]{0:T(512)(128)(4,1)S(1)} %iota_compare_fusion.2, f32[40,320]{1,0:T(8,128)S(1)} %convolution_add_fusion), kind=kOutput, calls=%fused_computation.107 | convolution fusion | flops 342036480 | bytes 10045480 | tf_op jit(solution)/shard_map/dot_general | solution.py:119
  456.0 21.5 %all-gather.11.cloned.1.call-done = bf16[256,8192]{1,0:T(8,128)(2,1)} async-done(((bf16[256,512]{1,0:T(8,128)(2,1)}), bf16[256,8192]{1,0:T(8,128)(2,1)}) %all-gather.11.cloned.1.call-update) | async-done | bytes 4194320 | tf_op jit(solution)/shard_map/all_gather | solution.py:79
  477.5 4.0 fusion.5
  481.5 5.8 all_gather.23
  487.3 0.3 fusion.56
  487.6 3.5 fusion.3
  491.2 0.6 copy-done.11
  491.8 1.0 fusion.19
  492.9 1.2 fusion.120
  494.1 1.6 convolution_convert_fusion
  495.7 6.7 convolution_bitcast_fusion
  502.4 97.3 %all-reduce.2.cloned.1.call-done = f32[40,5120]{1,0:T(8,128)} async-done(((f32[40,5120]{1,0:T(8,128)}), f32[40,5120]{1,0:T(8,128)}) %all-reduce.2.cloned.1.call-update) | async-done | bytes 819216 | tf_op jit(solution)/shard_map/psum | solution.py:122
  599.7 1.5 reshape.226
  601.3 0.4 multiply_reduce_fusion
  601.7 0.6 fusion.29
  602.3 0.2 broadcast_in_dim.45
  602.5 0.1 copy.45
  602.6 0.2 broadcast_in_dim.43
  602.8 0.1 copy.44
  603.0 1.2 fusion.28
  604.2 94.5 %reduce-scatter.8.cloned.1.call-done = f32[512,256]{0,1:T(8,128)} async-done(((f32[8192,256]{0,1:T(8,128)}), f32[512,256]{0,1:T(8,128)}) %reduce-scatter.8.cloned.1.call-update) | async-done | bytes 524304 | tf_op jit(solution)/shard_map/reduce_scatter | solution.py:92
  698.7 2.0 bitcast_add_fusion
  (71 shorter events, 0.6 us)
Async XLA Ops:
  7.2 69.2 %all-gather.5.cloned.1.call-start = ((), (), s32[]{:S(2)}) async-start(), calls=%async_computation.3 | async-start | bytes 3686400 | tf_op jit(solution)/shard_map/all_gather | solution.py:148
  7.9 3.5 copy-start.16
  7.9 3.6 copy-start.17
  7.9 148.5 %all-gather.7.cloned.1.call-start = ((), (), s32[]{:S(2)}) async-start(), calls=%async_computation.4 | async-start | bytes 5898240 | tf_op jit(solution)/shard_map/all_gather | solution.py:149
  8.7 2.8 copy-start.18
  8.7 67.7 %copy-start.5 = (bf16[40,5120]{1,0:T(8,128)(2,1)S(1)}, bf16[40,5120]{1,0:T(8,128)(2,1)}, u32[]{:S(2)}) copy-start(bf16[40,5120]{1,0:T(8,128)(2,1)} %param.16) | copy-start | bytes 1228804
  8.7 213.3 %reduce-scatter.4.cloned.1.call-start = ((), (), s32[]{:S(2)}) async-start(), calls=%async_computation.5 | async-start | bytes 1392640 | tf_op jit(solution)/shard_map/reduce_scatter | solution.py:110
  11.4 149.7 %copy-start = (f32[5,8,4,1280]{3,1,2,0:T(8,128)}, f32[5,8,4,1280]{3,1,2,0:T(8,128)S(1)}, u32[]{:S(2)}) copy-start(f32[5,8,4,1280]{3,1,2,0:T(8,128)S(1)} %copy.42) | copy-start | bytes 2457604
  79.4 82.4 %copy-start.19 = (bf16[512]{0:T(512)(128)(2,1)S(1)}, bf16[512]{0:T(512)(128)(2,1)}, u32[]{:S(2)}) copy-start(bf16[512]{0:T(512)(128)(2,1)} %param.22) | copy-start | bytes 3076
  79.4 82.5 %copy-start.8 = (bf16[2,8192]{1,0:T(2,128)(2,1)S(1)}, bf16[2,8192]{1,0:T(2,128)(2,1)}, u32[]{:S(2)}) copy-start(bf16[2,8192]{1,0:T(2,128)(2,1)} %param.27) | copy-start | bytes 98308
  79.4 82.5 %copy-start.20 = (s32[40]{0:T(128)S(1)}, s32[40]{0:T(128)}, u32[]{:S(2)}) copy-start(s32[40]{0:T(128)} %param.23) | copy-start | bytes 484
  161.1 127.0 %all-gather.9.cloned.1.call-start = ((), (), s32[]{:S(2)}) async-start(), calls=%async_computation.6 | async-start | bytes 4456448 | tf_op jit(solution)/shard_map/all_gather | solution.py:79
  252.0 158.9 %reduce-scatter.6.cloned.1.call-start = ((), (), s32[]{:S(2)}) async-start(), calls=%async_computation.7 | async-start | bytes 8912896 | tf_op jit(solution)/shard_map/reduce_scatter | solution.py:92
  257.8 6.4 copy-start.15
  264.4 39.0 %copy-start.9 = (pred[256,256]{0,1:T(8,128)(4,1)}, pred[256,256]{0,1:T(8,128)(4,1)S(1)}, u32[]{:S(2)}) copy-start(pred[256,256]{0,1:T(8,128)(4,1)S(1)} %fusion.36) | copy-start | bytes 196612
  288.1 10.2 %copy-start.4 = (bf16[256,8192]{1,0:T(8,128)(2,1)S(1)}, bf16[256,8192]{1,0:T(8,128)(2,1)}, u32[]{:S(2)}) copy-start(bf16[256,8192]{1,0:T(8,128)(2,1)} %copy.26) | copy-start | bytes 12582916
  298.2 3.6 copy-start.13
  298.2 3.6 copy-start.14
  301.8 0.6 copy-start.12
  313.0 164.4 %all-gather.11.cloned.1.call-start = ((), (), s32[]{:S(2)}) async-start(), calls=%async_computation.8 | async-start | bytes 4456448 | tf_op jit(solution)/shard_map/all_gather | solution.py:79
  441.6 158.2 %all-reduce.2.cloned.1.call-start = ((), (), s32[]{:S(2)}) async-start(), calls=%async_computation.10 | async-start | bytes 1638400 | tf_op jit(solution)/shard_map/psum | solution.py:122
  441.8 6.5 copy-start.7
  455.9 242.8 %reduce-scatter.8.cloned.1.call-start = ((), (), s32[]{:S(2)}) async-start(), calls=%async_computation.9 | async-start | bytes 8912896 | tf_op jit(solution)/shard_map/reduce_scatter | solution.py:92
  477.5 10.1 %copy-start.3 = (bf16[256,8192]{1,0:T(8,128)(2,1)S(1)}, bf16[256,8192]{1,0:T(8,128)(2,1)}, u32[]{:S(2)}) copy-start(bf16[256,8192]{1,0:T(8,128)(2,1)} %copy.30) | copy-start | bytes 12582916
  487.6 4.2 copy-start.10
  491.2 0.6 copy-start.11
  601.3 1.7 copy-start.1
  601.3 1.7 copy-start.6
  602.6 96.1 %copy-start.2 = (f32[512,256]{0,1:T(8,128)S(1)}, f32[512,256]{0,1:T(8,128)}, u32[]{:S(2)}) copy-start(f32[512,256]{0,1:T(8,128)} %reduce-scatter.6.cloned.1.call-done) | copy-start | bytes 1572868
Sparse Core Ops, SparseCore 0:
  10.4 65.9 all-gather.4
  78.6 77.7 all-gather.6
  161.2 60.7 reduce-scatter.3
  252.1 35.9 all-gather.8
  313.2 97.6 reduce-scatter.5
  441.7 35.7 all-gather.10
  480.5 119.1 all-reduce.1
  602.1 96.5 reduce-scatter.7
where the time goes:
time: 709 us; the launch traced here: 708 us
  waiting for transfers between devices  538 us (76%)
  blocking collectives  66.9 us (9%)
  matrix products  52.9 us (7%)
  local copies, waits for them, and re-layouts  24.3 us (3%)
  between operations  15.3 us (2%)
  other arithmetic  9.97 us (1%)
    reduce_scatter x2, waiting for transfers between devices, section_features(): lax.psum_scatter(lax.dot_general(o_local, attended, (((0,), (1,)), ((), (...  192 us
    psum x1, waiting for transfers between devices, merger_back(): normed_grads = lax.psum(normed_grads, ('sec', 'mp'))  97.3 us
    all_gather x1, waiting for transfers between devices, local(): lax.all_gather(w_out, 'dp', axis=1, tiled=True)  77 us
    all_gather x1, waiting for transfers between devices, local(): lax.all_gather(w_in, 'dp', axis=0, tiled=True)  64.8 us
    reduce_scatter x1, waiting for transfers between devices, merger_front(): lax.psum_scatter(partial_out, ('sec', 'mp'), scatter_dimension=1, tiled=T...  60 us
    psum x2, blocking collectives, section_features(): lax.psum(jnp.sum(rows_local * rows_local, axis=1), ('sec', 'mp'))  55.3 us
    all_gather x2, waiting for transfers between devices, gather_features(): return lax.all_gather(rows_local, ('sec', 'mp'), axis=1, tiled=True)  44.8 us
    dot_general x3, local copies, waits for them, and re-layouts, attend(): jnp.dot(normed, q_local, preferred_element_type=jnp.float32)  18.6 us
  transfers between devices with their start and end apart: 8, of which 8 were waited for; matrix products, arithmetic and copies ran while one was open for 8% of the time, Pallas kernels for 0%

commit v1 on v0

v1 whole, which is shorter than its diff:
```python
import functools
import math

import jax
import jax.numpy as jnp
from jax import lax
from jax.experimental import pallas as pl
from jax.experimental.pallas import tpu as pltpu
from jax.sharding import PartitionSpec as P

D = 8192
HEAD_DIM = 128
PAD = 48

ln_eps = 1e-06
rms_eps = 1e-06
rope_base = 1000000.0

MESH = pl.DeviceIdType.MESH
F32 = jnp.float32
BF16 = jnp.bfloat16


class Place:
    def __init__(self):
        self.y = lax.axis_index("sec")
        self.d = lax.axis_index("dp")
        mp = lax.axis_index("mp")
        self.mp = mp
        self.x = mp // 2
        self.c = lax.rem(mp, 2)
        self.yu = lax.rem(self.y + 1, 4)
        self.yd = lax.rem(self.y + 3, 4)
        self.ya = lax.rem(self.y + 2, 4)
        self.xo = 1 - self.x
        self.co = 1 - self.c
        self.U = self.dev(self.yu, self.x, self.c)
        self.Dn = self.dev(self.yd, self.x, self.c)
        self.X = self.dev(self.y, self.xo, self.c)
        self.C = self.dev(self.y, self.x, self.co)
        self.XC = self.dev(self.y, self.xo, self.co)
        self.me = self.sid(self.y, self.x, self.c)

    def dev(self, y, x, c):
        return {"sec": y, "dp": self.d, "mp": x * 2 + c}

    def sid(self, y, x, c):
        return y * 4 + x * 2 + c


def rcopy(src, dst, ssem, rsem, dev):
    return pltpu.make_async_remote_copy(
        src_ref=src, dst_ref=dst, send_sem=ssem, recv_sem=rsem, device_id=dev, device_id_type=MESH
    )


def barrier_with(devs):
    sem = pltpu.get_barrier_semaphore()
    for dev in devs:
        pl.semaphore_signal(sem, inc=1, device_id=dev, device_id_type=MESH)
    pl.semaphore_wait(sem, len(devs))


class Gather:
    def __init__(self, pl_, buf, rows, ssem, rsem):
        self.p, self.buf, self.half = pl_, buf, rows // 2
        self.ssem, self.rsem = ssem, rsem
        self.sent = []

    def view(self, s, h):
        return self.buf.at[s, pl.ds(h * self.half, self.half), :]

    def send(self, s, h, dev):
        k = len(self.sent)
        cp = rcopy(self.view(s, h), self.view(s, h), self.ssem.at[k], self.rsem.at[s * 2 + h], dev)
        cp.start()
        self.sent.append(cp)

    def wait(self, s, h):
        rcopy(
            self.view(s, h), self.view(s, h), self.ssem.at[0], self.rsem.at[s * 2 + h], self.p.C
        ).wait_recv()

    def wait_all(self, s):
        self.wait(s, 0)
        self.wait(s, 1)

    def start(self):
        p = self.p
        for h in range(2):
            for dev in (p.X, p.U, p.Dn, p.C):
                self.send(p.me, h, dev)

    def first(self):
        p = self.p
        for h in range(2):
            s = p.sid(p.y, p.xo, p.c)
            self.wait(s, h)
            self.send(s, h, p.U)
            self.send(s, h, p.Dn)
            self.send(s, h, p.C)
            s = p.sid(p.yd, p.x, p.c)
            self.wait(s, h)
            if h == 0:
                self.send(s, h, p.U)
            self.send(s, h, p.C)
            s = p.sid(p.yu, p.x, p.c)
            self.wait(s, h)
            if h == 1:
                self.send(s, h, p.Dn)
            self.send(s, h, p.C)

    def second(self):
        p = self.p
        s = p.sid(p.ya, p.x, p.c)
        for h in range(2):
            self.wait(s, h)
            self.send(s, h, p.X)
            self.send(s, h, p.C)
        for h in range(2):
            for y in (p.yd, p.yu):
                s = p.sid(y, p.xo, p.c)
                self.wait(s, h)
                self.send(s, h, p.C)

    def third(self):
        p = self.p
        s = p.sid(p.ya, p.xo, p.c)
        for h in range(2):
            self.wait(s, h)
            self.send(s, h, p.C)

    def drain(self):
        for cp in self.sent:
            cp.wait_send()


GATHER_SENDS = 30


class Scatter:
    def __init__(self, pl_, sb, rb, parts, ssem, rsem, piece):
        self.p, self.sb, self.rb, self.parts = pl_, sb, rb, parts
        self.ssem, self.rsem, self.piece = ssem, rsem, piece
        self.sent = []

    def copy(self, i, part, dev):
        return rcopy(
            self.sb.at[i].at[self.parts[part]],
            self.rb.at[i].at[self.parts[part]],
            self.ssem.at[i * 2 + part],
            self.rsem.at[i * 2 + part],
            dev,
        )

    def send(self, i, part, dev, value):
        self.sb.at[i][self.parts[part]] = value.astype(BF16)
        cp = self.copy(i, part, dev)
        cp.start()
        self.sent.append(cp)

    def got(self, i, part):
        self.copy(i, part, self.p.C).wait_recv()
        return self.rb.at[i][self.parts[part]].astype(F32)

    def first(self, part):
        p, piece = self.p, self.piece
        self.send(0, part, p.X, piece(p.ya, p.xo, part))
        self.send(1, part, p.U, piece(p.yu, p.xo, part))
        self.send(2, part, p.Dn, piece(p.yd, p.xo, part))
        if part == 1:
            self.send(5, 1, p.U, piece(p.yu, p.x, 1))
        else:
            self.send(6, 0, p.Dn, piece(p.yd, p.x, 0))

    def second(self, part):
        p, piece = self.p, self.piece
        own = piece(p.ya, p.x, part)
        self.send(3, part, p.U if part == 0 else p.Dn, own + self.got(0, part))
        own = piece(p.y, p.xo, part)
        self.send(4, part, p.X, own + self.got(1, part) + self.got(2, part))

    def third(self):
        p, piece = self.p, self.piece
        own = piece(p.yu, p.x, 0)
        self.send(5, 0, p.U, own + self.got(3, 0))
        own = piece(p.yd, p.x, 1)
        self.send(6, 1, p.Dn, own + self.got(3, 1))

    def last(self, part):
        p = self.p
        own = self.piece(p.y, p.x, part)
        return own + self.got(4, part) + self.got(5, part) + self.got(6, part)

    def drain(self):
        for cp in self.sent:
            cp.wait_send()


def norm_parts(group):
    center = group - jnp.mean(group, axis=-1, keepdims=True)
    spread = jnp.mean(center * center, axis=-1, keepdims=True)
    rstd = lax.rsqrt(spread + ln_eps)
    return center * rstd, rstd


def merger_kernel(
    count_ref,
    patches_ref,
    grads_ref,
    gain_ref,
    shift_ref,
    w_in_ref,
    b_in_ref,
    w_out_ref,
    b_out_ref,
    place_ref,
    text_ref,
    start_ref,
    pg_ref,
    xs,
    gs,
    xall,
    gall,
    psend,
    precv,
    hall,
    csend,
    crecv,
    pieces,
    sb,
    rb,
    fin,
    finr,
    gg,
    sx,
    rx,
    rg,
    sf,
    sp,
    rp,
    sh,
    rh,
    sc,
    rc,
    srs,
    rrs,
    sperm,
    rperm,
    sag,
    rag,
):
    p = Place()
    n_dp = xall.shape[0]
    rows = patches_ref.shape[0]
    vit = gain_ref.shape[1]
    groups = patches_ref.shape[1] // vit
    xw = xall.shape[2]
    gw = gall.shape[2]
    hid = w_in_ref.shape[1]
    half_out = gw // 2
    half_in = xw // 2
    fill = jnp.zeros((PAD - rows, 1), F32)

    def peer(k):
        d = lax.rem(p.d + k, n_dp)
        return d, {"sec": p.y, "dp": d, "mp": p.mp}

    s = p.me
    swap_dp = s // 2
    swap_s = 2 * p.d + lax.rem(s, 2)
    swap = {"sec": swap_s // 4, "dp": swap_dp, "mp": lax.rem(swap_s, 4)}
    stays = jnp.logical_and(swap_dp == p.d, swap_s == s)

    sem = pltpu.get_barrier_semaphore()
    for k in range(1, n_dp):
        pl.semaphore_signal(sem, inc=1, device_id=peer(k)[1], device_id_type=MESH)
    for dev in (p.U, p.Dn, p.X, p.C, swap):
        pl.semaphore_signal(sem, inc=1, device_id=dev, device_id_type=MESH)

    gain = gain_ref[...]
    shift = shift_ref[...]
    for g in range(groups):
        cols = slice(g * vit, (g + 1) * vit)
        unit, _ = norm_parts(patches_ref[:, cols].astype(F32))
        scaled = unit * gain + shift
        xs[:, cols] = jnp.concatenate([scaled, jnp.broadcast_to(fill, (PAD - rows, vit))], 0).astype(
            BF16
        )
    live = lax.broadcasted_iota(jnp.int32, (rows, 1), 0) < count_ref[0]
    step = 1024
    for at in range(0, grads_ref.shape[1], step):
        g = jnp.where(live, grads_ref[:, at : at + step].astype(F32), 0.0)
        gs[:, at : at + step] = jnp.concatenate(
            [g, jnp.broadcast_to(fill, (PAD - rows, step))], 0
        ).astype(BF16)
    pl.semaphore_wait(sem, n_dp - 1 + 5)

    def xcopy(k):
        d, dev = peer(k)
        src = xs.at[:, pl.ds(pl.multiple_of(d * xw, 128), xw)]
        return rcopy(src, xall.at[p.d], sx.at[k], rx.at[p.d], dev)

    def gcopy(k):
        d, dev = peer(k)
        src = gs.at[:, pl.ds(pl.multiple_of(d * gw, 128), gw)]
        return rcopy(src, gall.at[p.d], sx.at[k], rg.at[p.d], dev)

    def xfwd(k):
        d, _ = peer(k)
        return rcopy(xall.at[d], xall.at[d], sf.at[k], rx.at[d], p.C)

    def gfwd(k):
        d, _ = peer(k)
        return rcopy(gall.at[d], gall.at[d], sf.at[k], rg.at[d], p.C)

    ks = list(range(1, n_dp))

    @pl.when(p.c == 0)
    def _():
        for k in ks:
            xcopy(k).start()

    @pl.when(p.c == 1)
    def _():
        for k in ks:
            gcopy(k).start()

    xall[p.d] = xs[:, pl.ds(pl.multiple_of(p.d * xw, 128), xw)]
    gall[p.d] = gs[:, pl.ds(pl.multiple_of(p.d * gw, 128), gw)]

    @pl.when(p.c == 0)
    def _():
        for k in ks:
            xfwd(k).wait_recv()
            xfwd(k).start()
        for k in ks:
            gfwd(k).wait_recv()
        for k in ks:
            xcopy(k).wait_send()
            xfwd(k).wait_send()

    @pl.when(p.c == 1)
    def _():
        for k in ks:
            gfwd(k).wait_recv()
            gfwd(k).start()
        for k in ks:
            xfwd(k).wait_recv()
        for k in ks:
            gcopy(k).wait_send()
            gfwd(k).wait_send()

    flat = n_dp * PAD
    pf = jnp.dot(xall[...].reshape(flat, xw), w_in_ref[...], preferred_element_type=F32)
    psend[:, 0:PAD, :] = pf.astype(BF16).reshape(n_dp, PAD, hid)
    ph = lax.dot_general(
        gall[...].reshape(flat, gw),
        w_out_ref[...],
        (((1,), (1,)), ((), ())),
        preferred_element_type=F32,
    )
    psend[:, PAD:, :] = ph.astype(BF16).reshape(n_dp, PAD, hid)

    def pcopy(k):
        d, dev = peer(k)
        return rcopy(psend.at[d], precv.at[p.d], sp.at[k], rp.at[p.d], dev)

    def pwait(k):
        d, dev = peer(k)
        return rcopy(psend.at[d], precv.at[d], sp.at[k], rp.at[d], dev)

    for k in ks:
        pcopy(k).start()
    total = psend[p.d].astype(F32)
    for k in ks:
        pwait(k).wait_recv()
        total = total + precv[peer(k)[0]].astype(F32)
    for k in ks:
        pcopy(k).wait_send()

    pre_act = total[0:PAD] + b_in_ref[...]
    hidden_grads = total[PAD:]
    cdf = 0.5 * (1.0 + lax.erf(pre_act * (1.0 / math.sqrt(2.0))))
    pdf = jnp.exp(-0.5 * pre_act * pre_act) * (1.0 / math.sqrt(2.0 * math.pi))
    hall[p.d] = jnp.concatenate(
        [pre_act * cdf, hidden_grads * (cdf + pre_act * pdf)], axis=0
    ).astype(BF16)

    def hcopy(k):
        _, dev = peer(k)
        return rcopy(hall.at[p.d], hall.at[p.d], sh.at[k], rh.at[p.d], dev)

    def hwait(k):
        d, dev = peer(k)
        return rcopy(hall.at[d], hall.at[d], sh.at[k], rh.at[d], dev)

    for k in ks:
        hcopy(k).start()
    for k in ks:
        hwait(k).wait_recv()
    for k in ks:
        hcopy(k).wait_send()

    hidden = hall[:, 0:PAD, :].reshape(flat, hid)
    grads = hall[:, PAD:, :].reshape(flat, hid)

    def halves(c):
        m = jnp.dot(
            hidden,
            w_out_ref[:, pl.ds(pl.multiple_of(c * half_out, 128), half_out)],
            preferred_element_type=F32,
        )
        g = lax.dot_general(
            grads,
            w_in_ref[pl.ds(pl.multiple_of(c * half_in, 16), half_in), :],
            (((1,), (1,)), ((), ())),
            preferred_element_type=F32,
        )
        return m.reshape(n_dp, PAD, half_out), g.reshape(n_dp, PAD, half_in)

    wide = csend.shape[2]
    spare = jnp.zeros((n_dp, PAD, wide - half_out - half_in), F32)
    m, g = halves(p.co)
    csend[:, :, 0:half_out] = m.astype(BF16)
    csend[:, :, half_out:] = jnp.concatenate([g, spare], axis=2).astype(BF16)
    to_core = rcopy(csend, crecv, sc, rc, p.C)
    to_core.start()
    m, g = halves(p.c)
    pieces[:, :, 0:half_out] = m
    pieces[:, :, half_out:] = jnp.concatenate([g, spare], axis=2)
    to_core.wait_recv()
    parts = ((slice(None), slice(0, half_out)), (slice(None), slice(half_out, wide)))

    def piece(y, x, part):
        j = y * 2 + x
        rows_, cols_ = parts[part]
        return pieces[j, rows_, cols_] + crecv[j, rows_, cols_].astype(F32)

    rs = Scatter(p, sb, rb, parts, srs, rrs, piece)
    rs.first(0)
    rs.first(1)
    rs.second(0)
    rs.second(1)
    rs.third()
    for part in range(2):
        fin[parts[part]] = rs.last(part)

    over = rcopy(fin, finr, sperm, rperm, swap)

    @pl.when(stays)
    def _():
        finr[...] = fin[...]

    @pl.when(jnp.logical_not(stays))
    def _():
        over.start()

    to_core.wait_send()
    rs.drain()

    @pl.when(jnp.logical_not(stays))
    def _():
        over.wait_recv()
        over.wait_send()

    gg[p.me] = finr[:, half_out : half_out + half_in]
    ag = Gather(p, gg, PAD, sag, rag)
    ag.start()

    merged = (finr[0:rows, 0:half_out] + b_out_ref[...]).astype(BF16)
    tokens = text_ref.shape[0]
    token = lax.broadcasted_iota(jnp.int32, (tokens, rows), 0)
    slot = lax.broadcasted_iota(jnp.int32, (tokens, rows), 1)
    select = jnp.where(
        jnp.logical_and(place_ref[...] == token, slot < count_ref[0]), 1.0, 0.0
    ).astype(F32)
    image = jnp.sum(select, axis=1, keepdims=True)
    picked = jnp.dot(select.astype(BF16), merged, preferred_element_type=F32)
    start_ref[...] = jnp.where(image > 0.5, picked, text_ref[...].astype(F32)).astype(BF16)

    ag.first()
    ag.second()
    ag.third()
    for j in range(8):
        ag.wait_all(p.sid(j // 2, lax.rem(j, 2), p.co))
    ag.drain()
    per = vit // half_in
    for g in range(groups):
        cols = slice(g * vit, (g + 1) * vit)
        unit, rstd = norm_parts(patches_ref[:, cols].astype(F32))
        down = jnp.concatenate([gg[g * per + i] for i in range(per)], axis=1)[0:rows] * gain
        mean = jnp.mean(down, axis=-1, keepdims=True)
        along = jnp.mean(down * unit, axis=-1, keepdims=True)
        pg_ref[:, cols] = rstd * (down - mean - unit * along)


def merger(count, patches, grads, gain, shift, w_in, b_in, w_out, b_out, place, text):
    n_dp = 8
    xw, gw, hid = w_in.shape[0], w_out.shape[1], w_in.shape[1]
    wide = gw // 2 + ((xw // 2 + 127) // 128) * 128
    dma = pltpu.SemaphoreType.DMA
    vm = pl.BlockSpec(memory_space=pltpu.VMEM)
    return pl.pallas_call(
        merger_kernel,
        out_shape=(
            jax.ShapeDtypeStruct(text.shape, BF16),
            jax.ShapeDtypeStruct(patches.shape, F32),
        ),
        in_specs=[pl.BlockSpec(memory_space=pltpu.SMEM)] + [vm] * 10,
        out_specs=(vm, vm),
        scratch_shapes=[
            pltpu.VMEM((PAD, patches.shape[1]), BF16),
            pltpu.VMEM((PAD, grads.shape[1]), BF16),
            pltpu.VMEM((n_dp, PAD, xw), BF16),
            pltpu.VMEM((n_dp, PAD, gw), BF16),
            pltpu.VMEM((n_dp, 2 * PAD, hid), BF16),
            pltpu.VMEM((n_dp, 2 * PAD, hid), BF16),
            pltpu.VMEM((n_dp, 2 * PAD, hid), BF16),
            pltpu.VMEM((n_dp, PAD, wide), BF16),
            pltpu.VMEM((n_dp, PAD, wide), BF16),
            pltpu.VMEM((n_dp, PAD, wide), F32),
            pltpu.VMEM((7, PAD, wide), BF16),
            pltpu.VMEM((7, PAD, wide), BF16),
            pltpu.VMEM((PAD, wide), F32),
            pltpu.VMEM((PAD, wide), F32),
            pltpu.VMEM((16, PAD, xw // 2), F32),
            dma((n_dp,)),
            dma((n_dp,)),
            dma((n_dp,)),
            dma((n_dp,)),
            dma((n_dp,)),
            dma((n_dp,)),
            dma((n_dp,)),
            dma((n_dp,)),
            dma,
            dma,
            dma((14,)),
            dma((14,)),
            dma,
            dma,
            dma((GATHER_SENDS,)),
            dma((32,)),
        ],
        compiler_params=pltpu.CompilerParams(
            collective_id=0, has_side_effects=True, vmem_limit_bytes=48 * 2**20
        ),
    )(count, patches, grads, gain, shift, w_in, b_in, w_out, b_out, place, text)


def layers_kernel(
    start_ref,
    gain_ref,
    inv_ref,
    mask_ref,
    cos_ref,
    sin_ref,
    cos_t_ref,
    sin_t_ref,
    q_hbm,
    kv_hbm,
    o_hbm,
    out_ref,
    gath,
    qv,
    kvv,
    wv,
    acc_q,
    acc_kv,
    acc_ss,
    qb,
    kvx,
    attb,
    sb,
    rb,
    lq,
    lkv,
    lo,
    so,
    ro,
    sag,
    rag,
    skv,
    rkv,
    sat,
    rat,
    srs,
    rrs,
):
    p = Place()
    layers = q_hbm.shape[0]
    tokens = start_ref.shape[0]
    share = start_ref.shape[1]
    half = tokens // 2
    barrier_with((p.U, p.Dn, p.X, p.C, p.XC))

    def block(l, s):
        return pl.ds(pl.multiple_of(s * share, 128), share)

    def loads(l):
        out = [
            pltpu.make_async_copy(q_hbm.at[l], qv.at[l], lq.at[l]),
            pltpu.make_async_copy(kv_hbm.at[l, 0], kvv.at[l, 0], lkv.at[l, 0]),
            pltpu.make_async_copy(kv_hbm.at[l, 1], kvv.at[l, 1], lkv.at[l, 1]),
        ]
        return out

    rows_of = pl.ds(pl.multiple_of(p.c * 256, 16), 256)

    def own_o(l, j):
        s = p.sid(j // 2, lax.rem(j, 2), p.c)
        return pltpu.make_async_copy(
            o_hbm.at[l, :, block(l, s)], wv.at[l, j, rows_of, :], lo.at[l, j]
        )

    def give_o(l, j):
        s = p.sid(j // 2, lax.rem(j, 2), p.co)
        return rcopy(
            o_hbm.at[l, :, block(l, s)],
            wv.at[l, j, rows_of, :],
            so.at[l, j],
            ro.at[l, j],
            p.C,
        )

    for cp in loads(0):
        cp.start()
    out_ref[...] = start_ref[...].astype(F32)

    def layer(l, carry):
        gain = gain_ref[l, :, block(l, p.me)]
        gath[p.me] = (out_ref[...] * gain).astype(BF16)
        ag = Gather(p, gath, tokens, sag, rag)
        ag.start()

        @pl.when(l == 0)
        def _():
            for j in range(8):
                own_o(0, j).start()
                give_o(0, j).start()
            for k in range(1, layers):
                for cp in loads(k):
                    cp.start()
                for j in range(8):
                    own_o(k, j).start()
                    give_o(k, j).start()

        acc_q[...] = jnp.zeros_like(acc_q)
        acc_kv[...] = jnp.zeros_like(acc_kv)
        acc_ss[...] = jnp.zeros_like(acc_ss)
        for cp in loads(l):
            cp.wait()

        def project(s):
            g = gath[s]
            acc_q[...] += jnp.dot(g, qv[l, block(l, s), :], preferred_element_type=F32)
            for i in range(2):
                acc_kv[pl.ds(i * 32, 32), :] += lax.dot_general(
                    kvv[l, i, :, block(l, s)],
                    g,
                    (((1,), (1,)), ((), ())),
                    preferred_element_type=F32,
                )
            gf = g.astype(F32)
            sq = gf * gf * inv_ref[l, :, block(l, s)]
            fold = sq[:, 0:128]
            for at in range(128, share, 128):
                fold = fold + sq[:, at : at + 128]
            acc_ss[...] += fold

        project(p.me)
        ag.first()
        s = p.sid(p.y, p.x, p.co)
        ag.wait_all(s)
        project(s)
        project(p.sid(p.y, p.xo, p.c))
        ag.second()
        project(p.sid(p.yd, p.x, p.c))
        project(p.sid(p.yu, p.x, p.c))
        ag.third()
        for y, x in ((p.y, p.xo), (p.yd, p.x), (p.yu, p.x)):
            s = p.sid(y, x, p.co)
            ag.wait_all(s)
            project(s)
        for y, x in ((p.ya, p.x), (p.yd, p.xo), (p.yu, p.xo), (p.ya, p.xo)):
            project(p.sid(y, x, p.c))
        for y, x in ((p.ya, p.x), (p.yd, p.xo), (p.yu, p.xo), (p.ya, p.xo)):
            s = p.sid(y, x, p.co)
            ag.wait_all(s)
            project(s)

        total = jnp.sum(acc_ss[...], axis=1, keepdims=True)
        factor = lax.rsqrt(jnp.broadcast_to(total, (tokens, 128)) * (1.0 / D) + rms_eps)
        factor_t = jnp.transpose(factor)
        kvx[p.mp] = (acc_kv[...] * factor_t[0:64, :]).astype(BF16)

        def kv_copy(i, dev):
            return rcopy(kvx.at[p.mp], kvx.at[p.mp], skv.at[i], rkv.at[p.mp], dev)

        kv_to = [kv_copy(0, p.X), kv_copy(1, p.XC), kv_copy(2, p.C)]
        for cp in kv_to:
            cp.start()
        for hh in range(2):
            cols = slice(hh * 128, (hh + 1) * 128)
            q = acc_q[:, cols] * factor
            qb[:, cols] = (q * cos_ref[...] + pltpu.roll(q, 64, 1) * sin_ref[...]).astype(BF16)
        ag.drain()
        for m in (p.xo * 2 + p.c, p.xo * 2 + p.co, p.x * 2 + p.co):
            rcopy(kvx.at[m], kvx.at[m], skv.at[0], rkv.at[m], p.C).wait_recv()
        low = jnp.concatenate([kvx[0, 0:32, :], kvx[1, 0:32, :]], axis=0).astype(F32)
        high = jnp.concatenate([kvx[2, 0:32, :], kvx[3, 0:32, :]], axis=0).astype(F32)
        cos_t, sin_t = cos_t_ref[...], sin_t_ref[...]
        keys = jnp.concatenate(
            [low * cos_t - high * sin_t, high * cos_t + low * sin_t], axis=0
        ).astype(BF16)
        values = jnp.concatenate([kvx[m, 32:64, :] for m in range(4)], axis=0)

        def attend(part):
            rows = slice(part * half, (part + 1) * half)
            seen = (part + 1) * half
            for hh in range(2):
                cols = slice(hh * 128, (hh + 1) * 128)
                scores = jnp.dot(qb[rows, cols], keys[:, 0:seen], preferred_element_type=F32) * (
                    1.0 / math.sqrt(HEAD_DIM)
                )
                scores = jnp.where(mask_ref[rows, 0:seen] > 0.5, scores, -1e30)
                top = jnp.max(scores, axis=-1, keepdims=True)
                weights = jnp.exp(scores - top)
                weights = (weights / jnp.sum(weights, axis=-1, keepdims=True)).astype(BF16)
                attb[p.c, rows, cols] = lax.dot_general(
                    weights,
                    values[:, 0:seen],
                    (((1,), (1,)), ((), ())),
                    preferred_element_type=F32,
                ).astype(BF16)

        def at_copy(part, c):
            view = attb.at[c, pl.ds(part * half, half), :]
            return rcopy(view, view, sat.at[part], rat.at[part], p.C)

        for j in range(8):
            own_o(l, j).wait()
            give_o(l, j).wait_recv()

        def piece(y, x, part):
            j = y * 2 + x
            rows = pl.ds(part * half, half)
            return jnp.dot(
                attb[0, rows, :], wv[l, j, 0:256, :], preferred_element_type=F32
            ) + jnp.dot(attb[1, rows, :], wv[l, j, 256:512, :], preferred_element_type=F32)

        parts = tuple((slice(i * half, (i + 1) * half), slice(None)) for i in range(2))
        rs = Scatter(p, sb, rb, parts, srs, rrs, piece)
        for part in range(2):
            attend(part)
            at_copy(part, p.c).start()
        for part in range(2):
            at_copy(part, p.co).wait_recv()
            rs.first(part)
        rs.second(0)
        rs.second(1)
        rs.third()
        for part in range(2):
            rows = parts[part][0]
            out_ref[rows, :] += rs.last(part)
        rs.drain()
        for cp in kv_to:
            cp.wait_send()
        for part in range(2):
            at_copy(part, p.c).wait_send()
        for j in range(8):
            give_o(l, j).wait_send()
        return carry

    lax.fori_loop(0, layers, layer, 0)


def layers_call(start, gain, inv, mask, cos, sin, cos_t, sin_t, q_weight, kv_weight, o_weight):
    tokens, share = start.shape
    layers = q_weight.shape[0]
    dma = pltpu.SemaphoreType.DMA
    vm = pl.BlockSpec(memory_space=pltpu.VMEM)
    hbm = pl.BlockSpec(memory_space=pl.ANY)
    return pl.pallas_call(
        layers_kernel,
        out_shape=jax.ShapeDtypeStruct((tokens, share), F32),
        in_specs=[vm] * 8 + [hbm] * 3,
        out_specs=vm,
        scratch_shapes=[
            pltpu.VMEM((16, tokens, share), BF16),
            pltpu.VMEM(q_weight.shape, BF16),
            pltpu.VMEM(kv_weight.shape, BF16),
            pltpu.VMEM((layers, 8, 512, share), BF16),
            pltpu.VMEM((tokens, 256), F32),
            pltpu.VMEM((64, tokens), F32),
            pltpu.VMEM((tokens, 128), F32),
            pltpu.VMEM((tokens, 256), BF16),
            pltpu.VMEM((4, 64, tokens), BF16),
            pltpu.VMEM((2, tokens, 256), BF16),
            pltpu.VMEM((7, tokens, share), BF16),
            pltpu.VMEM((7, tokens, share), BF16),
            dma((layers,)),
            dma((layers, 2)),
            dma((layers, 8)),
            dma((layers, 8)),
            dma((layers, 8)),
            dma((GATHER_SENDS,)),
            dma((32,)),
            dma((3,)),
            dma((4,)),
            dma((2,)),
            dma((2,)),
            dma((14,)),
            dma((14,)),
        ],
        compiler_params=pltpu.CompilerParams(
            collective_id=1, has_side_effects=True, vmem_limit_bytes=60 * 2**20
        ),
    )(start, gain, inv, mask, cos, sin, cos_t, sin_t, q_weight, kv_weight, o_weight)


def local(
    patches,
    ln_gain,
    ln_shift,
    w_in,
    b_in,
    w_out,
    b_out,
    place,
    image_counts,
    text_rows,
    segments,
    norm_gain,
    q_weight,
    kv_weight,
    o_weight,
    grad_rows,
):
    start, patch_grads = merger(
        image_counts,
        patches,
        grad_rows,
        ln_gain.astype(F32)[None],
        ln_shift.astype(F32)[None],
        w_in,
        b_in.astype(F32)[None],
        w_out,
        b_out.astype(F32)[None],
        place[None],
        text_rows,
    )
    tokens = text_rows.shape[0]
    index = jnp.arange(tokens, dtype=jnp.int32)
    ids = segments[0]
    allowed = (ids[:, None] == ids[None, :]) & (index[None, :] <= index[:, None])
    mask = allowed.astype(F32)
    positions = jnp.sum(mask, axis=1) - 1.0
    half = HEAD_DIM // 2
    inv_freq = rope_base ** (-2.0 * jnp.arange(half, dtype=F32) / HEAD_DIM)
    angles = positions[:, None] * inv_freq[None, :]
    cos, sin = jnp.cos(angles), jnp.sin(angles)
    gain = norm_gain.astype(F32)[:, None, :]
    out = layers_call(
        start,
        gain,
        1.0 / (gain * gain),
        mask,
        jnp.concatenate([cos, cos], axis=1),
        jnp.concatenate([-sin, sin], axis=1),
        cos.T,
        sin.T,
        q_weight,
        kv_weight,
        o_weight,
    )
    return (out, patch_grads)


def solution(mesh):
    in_specs = (
        P("dp", None),
        P(),
        P(),
        P("dp", ("sec", "mp")),
        P(("sec", "mp")),
        P(("sec", "mp"), "dp"),
        P(("sec", "mp")),
        P("dp"),
        P("dp"),
        P("dp", ("sec", "mp")),
        P("dp", None),
        P(),
        P(None, None, ("sec", "mp")),
        P(None, None, ("sec", "mp"), None),
        P(None, ("sec", "mp"), None),
        P("dp", None),
    )
    out_specs = (P("dp", ("sec", "mp")), P("dp", None))
    return jax.shard_map(local, mesh=mesh, in_specs=in_specs, out_specs=out_specs, check_vma=False)
```

time: 709 us -> 206 us (0.29)
  waiting for transfers between devices: 538 us -> 0 us
  Pallas kernels: 0 us -> 184 us
  blocking collectives: 66.9 us -> 0 us
  matrix products: 52.9 us -> 0 us
  between operations: 15.3 us -> 1.34 us
  local copies, waits for them, and re-layouts: 24.3 us -> 12.9 us
    reduce_scatter x3 -> x0, waiting for transfers between devices: 252 us -> none  [the longest x2 192 us: section_features(): lax.psum_scatter(lax.dot_general(o_local, attended, (((0,), (1,)), ((), (...]
    all_gather x4 -> x0, waiting for transfers between devices: 187 us -> none  [the longest x1 77 us: local(): lax.all_gather(w_out, 'dp', axis=1, tiled=True)]
    pallas_call x0 -> x2, Pallas kernels: none -> 184 us  [the longest x1 102 us: layers_call(): pl.pallas_call(layers_kernel, out_shape=jax.ShapeDtypeStruct((tokens, sha...]
    psum x1 -> x0, waiting for transfers between devices: 97.3 us -> none  [merger_back(): normed_grads = lax.psum(normed_grads, ('sec', 'mp'))]
    psum x2 -> x0, blocking collectives: 55.3 us -> none  [section_features(): lax.psum(jnp.sum(rows_local * rows_local, axis=1), ('sec', 'mp'))]
    dot_general x14 -> x0, matrix products: 50.5 us -> none  [the longest x2 13.4 us: section_features(): lax.dot_general(o_local, attended, (((0,), (1,)), ((), ())), preferred_el...]
    dot_general x3 -> x0, local copies, waits for them, and re-layouts: 18.6 us -> none  [attend(): jnp.dot(normed, q_local, preferred_element_type=jnp.float32)]
    all_gather x2 -> x0, blocking collectives: 11.6 us -> none  [attend(): key_value = lax.all_gather(key_value, 'mp', axis=2, tiled=True)]
  transfers between devices with their start and end apart: 8 -> 0, of which waited for: 8 -> 0; matrix products, arithmetic and copies ran while one was open for 8% -> 0% of each run, Pallas kernels for 0% -> 0%
where the time goes in v1:
time: 206 us; the launch traced here: 205 us
  Pallas kernels  184 us (89%)
  local copies, waits for them, and re-layouts  12.9 us (6%)
  other arithmetic  7.1 us (3%)
    pallas_call x1, Pallas kernels, layers_call(): pl.pallas_call(layers_kernel, out_shape=jax.ShapeDtypeStruct((tokens, sha...  102 us
    pallas_call x1, Pallas kernels, merger(): pl.pallas_call(merger_kernel, out_shape=(jax.ShapeDtypeStruct(text.shape,...  82.1 us
    unnamed x15, local copies, waits for them, and re-layouts  9.49 us

profile of v1, /device:TPU:0, one launch (start us, length us, event | category | flops | bytes accessed | tf_op | source)
XLA Modules:
  0.0 205.3 jit_solution(3196679170434178880)
XLA Ops:
  1.3 0.9 fusion.2
  2.2 0.7 reshape.17.b_in_ref
  2.9 0.7 broadcast_in_dim.43
  3.6 0.7 reshape.15.gain_ref
  4.3 0.7 reshape.16.shift_ref
  5.0 0.8 fusion.3
  5.8 0.7 div.18.inv_ref
  6.5 0.8 convert_bitcast_fusion
  7.3 0.7 copy.19.gain_ref
  7.9 1.0 multiply_sine_fusion.1
  8.9 1.6 fusion.1.mask_ref
  10.5 0.5 fusion.4
  11.0 0.8 pad_maximum_fusion
  11.8 1.3 copy.18.w_in_ref
  13.1 0.0 copy-start
  13.1 1.1 copy-done
  14.2 0.0 copy-start.1
  14.2 1.1 copy-done.1
  15.3 0.0 copy-start.2
  15.3 1.0 copy-done.2
  16.3 0.0 copy-start.4
  16.3 0.9 copy-done.4
  17.2 0.0 copy-start.5
  17.2 0.7 copy-done.5
  17.9 82.1 %shard_map.167 = (bf16[256,512]{1,0:T(8,128)(2,1)S(1)}, f32[40,5120]{1,0:T(8,128)S(1)}) custom-call(s32[1]{0:T(128)S(6)} %copy.22.count_ref, bf16[40,5120]{1,0:T(8,128)(2,1)S(1)} %copy-done.2, bf16[40,8192]{1,0:T(8,128)(2,1)S(1)} %copy-done, f32[1,1280]{1,0:T(1,128)S(1)} %reshape.15.gain_ref, f32[1,1280]{1,0:T(1,128)S(1)} %reshape.16.shift_ref, ...), custom_call_target="tpu_custom_call" | custom-call | tf_op jit(solution)/shard_map/pallas_call | solution.py:504
  100.0 0.0 copy-start.3
  100.0 0.7 copy-done.3
  100.7 101.9 %shard_map.168 = f32[256,512]{1,0:T(8,128)} custom-call(bf16[256,512]{1,0:T(8,128)(2,1)} %copy-done.3, f32[2,1,8192]{2,1,0:T(1,128)} %copy.19.gain_ref, f32[2,1,8192]{2,1,0:T(1,128)} %div.18.inv_ref, f32[256,256]{1,0:T(8,128)} %fusion.1.mask_ref, f32[256,128]{1,0:T(8,128)} %get-tuple-element.11.cos_ref, f32[256,128]{1,0:T(8,128)} %get-tuple-element.12.sin_ref, ...), custom_call_target="tpu_custom_call" | custom-call | tf_op jit(solution)/shard_map/pallas_call | solution.py:784
  202.6 1.9 copy.23
  204.4 0.9 copy.24
  (2 shorter events, 0.0 us)
Async XLA Ops:
  13.1 1.1 copy-start
  14.2 1.1 copy-start.1
  15.3 1.0 copy-start.2
  16.3 0.9 copy-start.4
  17.2 0.7 copy-start.5
  100.0 0.7 copy-start.3

commit v2 on v0

v2 whole, which is shorter than its diff:
```python
import functools
import math

import jax
import jax.numpy as jnp
from jax import lax
from jax.experimental import pallas as pl
from jax.experimental.pallas import tpu as pltpu
from jax.sharding import PartitionSpec as P

D = 8192
HEAD_DIM = 128
PAD = 48

ln_eps = 1e-06
rms_eps = 1e-06
rope_base = 1000000.0

MESH = pl.DeviceIdType.MESH
F32 = jnp.float32
BF16 = jnp.bfloat16


class Place:
    def __init__(self):
        self.y = lax.axis_index("sec")
        self.d = lax.axis_index("dp")
        mp = lax.axis_index("mp")
        self.mp = mp
        self.x = mp // 2
        self.c = lax.rem(mp, 2)
        self.yu = lax.rem(self.y + 1, 4)
        self.yd = lax.rem(self.y + 3, 4)
        self.ya = lax.rem(self.y + 2, 4)
        self.xo = 1 - self.x
        self.co = 1 - self.c
        self.U = self.dev(self.yu, self.x, self.c)
        self.Dn = self.dev(self.yd, self.x, self.c)
        self.X = self.dev(self.y, self.xo, self.c)
        self.C = self.dev(self.y, self.x, self.co)
        self.XC = self.dev(self.y, self.xo, self.co)
        self.me = self.sid(self.y, self.x, self.c)

    def dev(self, y, x, c):
        return {"sec": y, "dp": self.d, "mp": x * 2 + c}

    def sid(self, y, x, c):
        return y * 4 + x * 2 + c


def rcopy(src, dst, ssem, rsem, dev):
    return pltpu.make_async_remote_copy(
        src_ref=src, dst_ref=dst, send_sem=ssem, recv_sem=rsem, device_id=dev, device_id_type=MESH
    )


class Gather:
    def __init__(self, place, buf, chunks, ssem, rsem):
        self.p, self.buf, self.chunks = place, buf, chunks
        self.ssem, self.rsem = ssem, rsem
        self.sent = []

    def view(self, s, h):
        return self.buf.at[s].at[self.chunks[h]]

    def send(self, s, h, *devs):
        for dev in devs:
            k = len(self.sent)
            cp = rcopy(
                self.view(s, h), self.view(s, h), self.ssem.at[k], self.rsem.at[s * 2 + h], dev
            )
            cp.start()
            self.sent.append(cp)

    def wait(self, s, h):
        rcopy(
            self.view(s, h), self.view(s, h), self.ssem.at[0], self.rsem.at[s * 2 + h], self.p.C
        ).wait_recv()

    def wait_all(self, s):
        self.wait(s, 0)
        self.wait(s, 1)

    def steps(self, use):
        p = self.p
        own = p.c
        other = p.co

        def late(y, x):
            s = p.sid(y, x, other)
            self.wait_all(s)
            use(s)

        self.send(p.me, 0, p.X, p.U)
        self.send(p.me, 1, p.X, p.Dn)
        self.send(p.me, 1, p.U)
        self.send(p.me, 0, p.Dn, p.C)
        self.send(p.me, 1, p.C)
        use(p.me)
        yield 2.5
        up, down = p.sid(p.yu, p.x, own), p.sid(p.yd, p.x, own)
        self.wait(down, 0)
        self.send(down, 0, p.U, p.C)
        self.wait(up, 1)
        self.send(up, 1, p.Dn, p.C)
        yield 0.5
        beside = p.sid(p.y, p.xo, own)
        for h in range(2):
            self.wait(beside, h)
            self.send(beside, h, p.U, p.Dn, p.C)
        use(beside)
        yield 1.0
        self.wait(down, 1)
        self.send(down, 1, p.C)
        self.wait(up, 0)
        self.send(up, 0, p.C)
        use(down)
        use(up)
        late(p.y, p.x)
        yield 1.5
        far = p.sid(p.ya, p.x, own)
        for h in range(2):
            self.wait(far, h)
            self.send(far, h, p.X, p.C)
        use(far)
        late(p.y, p.xo)
        yield 1.0
        for y in (p.yd, p.yu):
            s = p.sid(y, p.xo, own)
            for h in range(2):
                self.wait(s, h)
                self.send(s, h, p.C)
            use(s)
        late(p.yd, p.x)
        late(p.yu, p.x)
        yield 1.0
        late(p.ya, p.x)
        s = p.sid(p.ya, p.xo, own)
        for h in range(2):
            self.wait(s, h)
            self.send(s, h, p.C)
        use(s)
        late(p.yd, p.xo)
        late(p.yu, p.xo)
        yield 1.0
        late(p.ya, p.xo)
        for cp in self.sent:
            cp.wait_send()


GATHER_SENDS = 30


class Scatter:
    def __init__(self, place, sb, rb, parts, ssem, rsem, piece):
        self.p, self.sb, self.rb, self.parts = place, sb, rb, parts
        self.ssem, self.rsem, self.piece = ssem, rsem, piece
        self.sent = []

    def copy(self, i, part, dev):
        return rcopy(
            self.sb.at[i].at[self.parts[part]],
            self.rb.at[i].at[self.parts[part]],
            self.ssem.at[i * 2 + part],
            self.rsem.at[i * 2 + part],
            dev,
        )

    def send(self, i, part, dev, value):
        self.sb.at[i][self.parts[part]] = value.astype(BF16)
        cp = self.copy(i, part, dev)
        cp.start()
        self.sent.append(cp)

    def both(self, i, dev, y, x):
        for part, value in enumerate(self.piece(y, x, None)):
            self.send(i, part, dev, value)

    def got(self, i, part):
        self.copy(i, part, self.p.C).wait_recv()
        return self.rb.at[i][self.parts[part]].astype(F32)

    def steps(self, finish, lag=1.0):
        p, piece = self.p, self.piece
        self.both(0, p.X, p.ya, p.xo)
        self.both(1, p.U, p.yu, p.xo)
        self.both(2, p.Dn, p.yd, p.xo)
        self.send(5, 1, p.U, piece(p.yu, p.x, 1))
        self.send(6, 0, p.Dn, piece(p.yd, p.x, 0))
        yield 2.0 * lag
        own = piece(p.ya, p.x, None)
        for part in range(2):
            self.send(3, part, (p.U, p.Dn)[part], own[part] + self.got(0, part))
        yield 1.0 * lag
        own = piece(p.y, p.xo, None)
        for part in range(2):
            self.send(4, part, p.X, own[part] + self.got(1, part) + self.got(2, part))
        yield 1.5 * lag
        own = piece(p.yu, p.x, 0)
        self.send(5, 0, p.U, own + self.got(3, 0))
        own = piece(p.yd, p.x, 1)
        self.send(6, 1, p.Dn, own + self.got(3, 1))
        yield 2.5 * lag
        own = piece(p.y, p.x, None)
        for part in range(2):
            finish(part, own[part] + self.got(4, part) + self.got(5, part) + self.got(6, part))
        for cp in self.sent:
            cp.wait_send()


def interleave(*streams):
    clock = [[start, i, stream] for i, (start, stream) in enumerate(streams)]
    while clock:
        now = min(clock, key=lambda item: (item[0], item[1]))
        try:
            now[0] += next(now[2])
        except StopIteration:
            clock.remove(now)


def norm_parts(group):
    center = group - jnp.mean(group, axis=-1, keepdims=True)
    spread = jnp.mean(center * center, axis=-1, keepdims=True)
    rstd = lax.rsqrt(spread + ln_eps)
    return center * rstd, rstd


VIT_AT, SHIFT_AT, B_OUT_AT, PLACE_AT, B_IN_AT = 0, 1280, 2560, 3072, 3200


def step_kernel(
    count_ref,
    small_ref,
    seg_ref,
    gain_ref,
    patches_hbm,
    grads_hbm,
    w_in_hbm,
    w_out_hbm,
    text_hbm,
    q_hbm,
    kv_hbm,
    o_hbm,
    out_ref,
    pg_ref,
    patches_ref,
    grads_ref,
    w_in_ref,
    w_out_ref,
    text_ref,
    lin,
    xs,
    gs,
    xall,
    gall,
    psend,
    precv,
    hall,
    pre_ref,
    fsend,
    frecv,
    fpiece,
    fsb,
    frb,
    bsend,
    brecv,
    bpiece,
    bsb,
    brb,
    ffin,
    ffinr,
    bfin,
    bfinr,
    gg,
    gimg,
    gath,
    qv,
    kvv,
    wv,
    gains,
    invs,
    mask_ref,
    cos_ref,
    sin_ref,
    cos_t_ref,
    sin_t_ref,
    acc_q,
    acc_kv,
    acc_ss,
    img_q,
    img_kv,
    img_ss,
    qb,
    kvx,
    attb,
    sb,
    rb,
    sx,
    rx,
    sf,
    sp,
    rp,
    sh,
    rh,
    sc,
    rc,
    srs,
    rrs,
    sperm,
    rperm,
    sag,
    rag,
    simg,
    rimg,
    lq,
    lkv,
    lo,
    so,
    ro,
    stx,
    rtx,
    skv,
    rkv,
    sat,
    rat,
    sls,
    rls,
):
    p = Place()
    n_dp = xall.shape[0]
    rows = patches_ref.shape[0]
    vit = 1280
    groups = patches_ref.shape[1] // vit
    xw, gw, hid = xall.shape[2], gall.shape[2], w_in_ref.shape[1]
    half_out, half_in = gw // 2, xw // 2
    layers = q_hbm.shape[0]
    tokens, share = text_ref.shape
    half = tokens // 2
    flat = n_dp * PAD
    ks = list(range(1, n_dp))

    def peer(k):
        d = lax.rem(p.d + k, n_dp)
        return d, {"sec": p.y, "dp": d, "mp": p.mp}

    swap_dp = p.me // 2
    swap_s = 2 * p.d + lax.rem(p.me, 2)
    swap = {"sec": swap_s // 4, "dp": swap_dp, "mp": lax.rem(swap_s, 4)}
    stays = jnp.logical_and(swap_dp == p.d, swap_s == p.me)
    moves = jnp.logical_not(stays)

    sem = pltpu.get_barrier_semaphore()
    for dev in [peer(k)[1] for k in ks] + [p.U, p.Dn, p.X, p.C, p.XC, swap]:
        pl.semaphore_signal(sem, inc=1, device_id=dev, device_id_type=MESH)

    def block(s):
        return pl.ds(pl.multiple_of(s * share, 128), share)

    def load(i):
        src, dst = (
            (patches_hbm, patches_ref),
            (text_hbm, text_ref),
            (w_in_hbm, w_in_ref),
            (w_out_hbm, w_out_ref),
            (grads_hbm, grads_ref),
        )[i]
        return pltpu.make_async_copy(src, dst, lin.at[i])

    def loads(l):
        return [
            pltpu.make_async_copy(q_hbm.at[l], qv.at[l], lq.at[l]),
            pltpu.make_async_copy(kv_hbm.at[l, 0], kvv.at[l, 0], lkv.at[l, 0]),
            pltpu.make_async_copy(kv_hbm.at[l, 1], kvv.at[l, 1], lkv.at[l, 1]),
        ]

    rows_of = pl.ds(pl.multiple_of(p.c * 256, 16), 256)

    def own_o(l, j):
        s = p.sid(j // 2, j % 2, p.c)
        return pltpu.make_async_copy(
            o_hbm.at[l, :, block(s)], wv.at[l, j, rows_of, :], lo.at[l, j]
        )

    def give_o(l, j):
        s = p.sid(j // 2, j % 2, p.co)
        return rcopy(
            o_hbm.at[l, :, block(s)], wv.at[l, j, rows_of, :], so.at[l, j], ro.at[l, j], p.C
        )

    for i in range(5):
        load(i).start()
    for cp in loads(0):
        cp.start()

    for l in range(layers):
        g = gain_ref[l : l + 1, :].astype(F32)
        gains[l] = g
        invs[l] = 1.0 / (g * g)
    ln_gain = small_ref[:, VIT_AT:SHIFT_AT]
    load(0).wait()
    for g in range(groups):
        cols = slice(g * vit, (g + 1) * vit)
        unit, _ = norm_parts(patches_ref[:, cols].astype(F32))
        scaled = unit * ln_gain + small_ref[:, SHIFT_AT:B_OUT_AT]
        xs[:, cols] = jnp.concatenate([scaled, jnp.zeros((PAD - rows, vit), F32)], 0).astype(BF16)
    load(1).wait()
    gain0 = gains[0, :, block(p.me)]
    for h in range(2):
        rows_h = slice(h * half, (h + 1) * half)
        gath[h, p.me] = (text_ref[rows_h, :].astype(F32) * gain0).astype(BF16)
    pl.semaphore_wait(sem, n_dp - 1 + 6)


    def spread(way, src, dst, width):
        def put(k):
            d, dev = peer(k)
            view = src.at[:, pl.ds(pl.multiple_of(d * width, 128), width)]
            return rcopy(view, dst.at[p.d], sx.at[way, k], rx.at[way, p.d], dev)

        def pass_on(k):
            d, _ = peer(k)
            return rcopy(dst.at[d], dst.at[d], sf.at[way, k], rx.at[way, d], p.C)

        def on_core(c, body):
            @pl.when(p.c == c)
            def _():
                body([k for k in ks if k % 2 == c])

        for c in range(2):
            on_core(c, lambda mine: [put(k).start() for k in mine])
        dst[p.d] = src[:, pl.ds(pl.multiple_of(p.d * width, 128), width)]
        yield 5.0
        for c in range(2):

            def arrive(mine):
                for k in mine:
                    pass_on(k).wait_recv()
                    pass_on(k).start()

            on_core(c, arrive)
        yield 1.5
        for c in range(2):

            def finish(mine):
                for k in ks:
                    if k not in mine:
                        pass_on(k).wait_recv()
                for k in mine:
                    put(k).wait_send()
                    pass_on(k).wait_send()

            on_core(c, finish)

    def back(way, term, done):
        psend[way] = term().astype(BF16).reshape(n_dp, PAD, hid)

        def put(k):
            d, dev = peer(k)
            return rcopy(
                psend.at[way, d], precv.at[way, p.d], sp.at[way, k], rp.at[way, p.d], dev
            )

        def take(k):
            d, dev = peer(k)
            return rcopy(psend.at[way, d], precv.at[way, d], sp.at[way, k], rp.at[way, d], dev)

        for k in ks:
            put(k).start()
        yield 6.0
        total = psend[way, p.d].astype(F32)
        for k in ks:
            take(k).wait_recv()
            total = total + precv[way, peer(k)[0]].astype(F32)
        done(total)
        for k in ks:
            put(k).wait_send()

    def share_units(way, value):
        hall[way, p.d] = value.astype(BF16)

        def put(k):
            return rcopy(
                hall.at[way, p.d], hall.at[way, p.d], sh.at[way, k], rh.at[way, p.d], peer(k)[1]
            )

        def take(k):
            d, dev = peer(k)
            return rcopy(hall.at[way, d], hall.at[way, d], sh.at[way, k], rh.at[way, d], dev)

        for k in ks:
            put(k).start()
        yield 5.0
        for k in ks:
            take(k).wait_recv()
        for k in ks:
            put(k).wait_send()

    def gather_sums(way, term, csend, crecv, pieces, s_buf, r_buf, fin, finr):
        csend[...] = term(p.co).astype(BF16)
        over = rcopy(csend, crecv, sc.at[way], rc.at[way], p.C)
        over.start()
        pieces[...] = term(p.c)
        yield 1.0
        over.wait_recv()
        wide = csend.shape[2]
        parts = ((slice(None), slice(0, 256)), (slice(None), slice(256, wide)))

        def piece(y, x, part):
            j = y * 2 + x
            out = []
            for r, c in parts:
                out.append(pieces[j, r, c] + crecv[j, r, c].astype(F32))
            return out if part is None else out[part]

        def finish(part, total):
            fin[parts[part]] = total.astype(fin.dtype)

        rs = Scatter(p, s_buf, r_buf, parts, srs.at[way], rrs.at[way], piece)
        yield from rs.steps(finish, 0.9)
        over.wait_send()
        cross = rcopy(fin, finr, sperm.at[way], rperm.at[way], swap)

        @pl.when(stays)
        def _():
            finr[...] = fin[...]

        @pl.when(moves)
        def _():
            cross.start()

        yield 4.0

        @pl.when(moves)
        def _():
            cross.wait_recv()
            cross.wait_send()

    def units(way):
        return hall[way].reshape(flat, hid)

    def forward():
        yield from spread(0, xs, xall, xw)
        load(2).wait()
        load(3).wait()

        def first():
            return jnp.dot(xall[...].reshape(flat, xw), w_in_ref[...], preferred_element_type=F32)

        def keep(total):
            pre_ref[...] = total + small_ref[:, B_IN_AT : B_IN_AT + hid]

        yield from back(0, first, keep)
        pre = pre_ref[...]
        yield from share_units(
            0, pre * 0.5 * (1.0 + lax.erf(pre * (1.0 / math.sqrt(2.0))))
        )

        def second(c):
            at = pl.ds(pl.multiple_of(c * half_out, 128), half_out)
            out = jnp.dot(units(0), w_out_ref[:, at], preferred_element_type=F32)
            return out.reshape(n_dp, PAD, half_out)

        yield from gather_sums(0, second, fsend, frecv, fpiece, fsb, frb, ffin, ffinr)
        merged = ffinr[...].astype(F32) + small_ref[:, B_OUT_AT:PLACE_AT]
        merged = merged.astype(BF16)
        gimg[p.me] = (merged.astype(F32) * gain0).astype(BF16)
        img_q[...] = jnp.zeros_like(img_q)
        img_kv[...] = jnp.zeros_like(img_kv)
        img_ss[...] = jnp.zeros_like(img_ss)
        chunks = tuple((slice(None), slice(i * 256, (i + 1) * 256)) for i in range(2))
        ag = Gather(p, gimg, chunks, simg, rimg)
        steps = ag.steps(lambda s: project(0, s, gimg[s], img_q, img_kv, img_ss))
        yield next(steps)
        for h in range(2):
            rows_h = slice(h * half, (h + 1) * half)
            chosen = select(h)
            picked = jnp.dot(chosen.astype(BF16), merged[0:rows], preferred_element_type=F32)
            image = jnp.sum(chosen, axis=1, keepdims=True) > 0.5
            out_ref[rows_h, :] = jnp.where(image, picked, text_ref[rows_h, :].astype(F32))
        yield from steps

    def backward():
        load(4).wait()
        live = lax.broadcasted_iota(jnp.int32, (rows, 1), 0) < count_ref[0]
        for at in range(0, gs.shape[1], 1024):
            g = jnp.where(live, grads_ref[:, at : at + 1024].astype(F32), 0.0)
            gs[:, at : at + 1024] = jnp.concatenate(
                [g, jnp.zeros((PAD - rows, 1024), F32)], 0
            ).astype(BF16)
        yield from spread(1, gs, gall, gw)
        box = []

        def first():
            return lax.dot_general(
                gall[...].reshape(flat, gw),
                w_out_ref[...],
                (((1,), (1,)), ((), ())),
                preferred_element_type=F32,
            )

        def keep(total):
            pre = pre_ref[...]
            cdf = 0.5 * (1.0 + lax.erf(pre * (1.0 / math.sqrt(2.0))))
            pdf = jnp.exp(-0.5 * pre * pre) * (1.0 / math.sqrt(2.0 * math.pi))
            box.append(total * (cdf + pre * pdf))

        yield from back(1, first, keep)
        yield from share_units(1, box[0])
        wide = bpiece.shape[2]

        def second(c):
            at = pl.ds(pl.multiple_of(c * half_in, 16), half_in)
            out = lax.dot_general(
                units(1), w_in_ref[at, :], (((1,), (1,)), ((), ())), preferred_element_type=F32
            ).reshape(n_dp, PAD, half_in)
            return jnp.concatenate([out, jnp.zeros((n_dp, PAD, wide - half_in), F32)], axis=2)

        yield from gather_sums(1, second, bsend, brecv, bpiece, bsb, brb, bfin, bfinr)
        gg[p.me] = bfinr[...]
        chunks = ((slice(None), slice(0, 256)), (slice(None), slice(256, wide)))
        yield from Gather(p, gg, chunks, sag, rag).steps(lambda s: None)
        per = vit // half_in
        for g in range(groups):
            cols = slice(g * vit, (g + 1) * vit)
            unit, rstd = norm_parts(patches_ref[:, cols].astype(F32))
            down = [gg[g * per + i, 0:rows, 0:half_in].astype(F32) for i in range(per)]
            down = jnp.concatenate(down, axis=1) * ln_gain
            mean = jnp.mean(down, axis=-1, keepdims=True)
            along = jnp.mean(down * unit, axis=-1, keepdims=True)
            pg_ref[:, cols] = rstd * (down - mean - unit * along)


    def project(l, s, g, q, kv, ss):
        q[...] += jnp.dot(g, qv[l, block(s), :], preferred_element_type=F32)
        for i in range(2):
            kv[pl.ds(i * 32, 32), :] += lax.dot_general(
                kvv[l, i, :, block(s)], g, (((1,), (1,)), ((), ())), preferred_element_type=F32
            )
        gf = g.astype(F32)
        sq = gf * gf * invs[l, :, block(s)]
        fold = sq[:, 0:128]
        for at in range(128, share, 128):
            fold = fold + sq[:, at : at + 128]
        ss[...] += fold

    def select(h):
        token = lax.broadcasted_iota(jnp.int32, (half, rows), 0) + h * half
        slot = lax.broadcasted_iota(jnp.int32, (half, rows), 1)
        at = small_ref[:, PLACE_AT : PLACE_AT + rows]
        hit = jnp.logical_and(at == token.astype(F32), slot < count_ref[0])
        return jnp.where(hit, 1.0, 0.0).astype(F32)

    def tables():
        ids = seg_ref[...].astype(F32)
        down = jnp.transpose(jnp.broadcast_to(ids, (128, tokens)))[:, 0:1]
        t = lax.broadcasted_iota(jnp.int32, (tokens, tokens), 0)
        s = lax.broadcasted_iota(jnp.int32, (tokens, tokens), 1)
        seen = jnp.where(jnp.logical_and(down == ids, s <= t), 1.0, 0.0).astype(F32)
        mask_ref[...] = seen
        position = jnp.sum(seen, axis=1, keepdims=True) - 1.0
        lane = lax.broadcasted_iota(jnp.int32, (1, HEAD_DIM), 1)
        low = lane < HEAD_DIM // 2
        order = jnp.where(low, lane, lane - HEAD_DIM // 2).astype(F32)
        angles = position * jnp.exp(order * (-2.0 * math.log(rope_base) / HEAD_DIM))
        cos, sin = jnp.cos(angles), jnp.sin(angles)
        cos_ref[...] = cos
        sin_ref[...] = jnp.where(low, -sin, sin)
        cos_t_ref[...] = jnp.transpose(cos)[0:64, :]
        sin_t_ref[...] = jnp.transpose(sin)[0:64, :]

    halves = tuple((slice(i * (half // 2), (i + 1) * (half // 2)), slice(None)) for i in range(2))

    def gather_rows(l, h):
        acc_q[h] = jnp.zeros_like(acc_q[h])
        acc_kv[h] = jnp.zeros_like(acc_kv[h])
        acc_ss[h] = jnp.zeros_like(acc_ss[h])

        def use(s):
            project(l, s, gath[h, s], acc_q.at[h], acc_kv.at[h], acc_ss.at[h])

        yield from Gather(p, gath.at[h], halves, stx.at[h], rtx.at[h]).steps(use)

    def text(h):
        if h == 0:
            for cp in loads(0):
                cp.wait()
        yield from gather_rows(0, h)
        if h == 1:
            tables()

    state = {}

    def attention(l, h):
        rows_h = slice(h * half, (h + 1) * half)
        if l == 0:
            chosen = select(h)
            image = jnp.sum(chosen, axis=1, keepdims=True) > 0.5
            exact = lax.Precision.HIGHEST
            for acc, img in ((acc_q, img_q), (acc_ss, img_ss)):
                put = jnp.dot(
                    chosen, img[0:rows, :], preferred_element_type=F32, precision=exact
                )
                acc[h] = jnp.where(image, put, acc[h])
            sides = (((1,), (1,)), ((), ()))
            put = lax.dot_general(
                img_kv[:, 0:rows], chosen, sides, preferred_element_type=F32, precision=exact
            )
            ones = jnp.ones((8, rows), F32)
            row = lax.dot_general(ones, chosen, sides, preferred_element_type=F32)[0:1, :]
            acc_kv[h] = jnp.where(row > 0.5, put, acc_kv[h])
        total = jnp.sum(acc_ss[h], axis=1, keepdims=True)
        factor = lax.rsqrt(jnp.broadcast_to(total, (half, 128)) * (1.0 / D) + rms_eps)
        factor_t = jnp.transpose(factor)
        kvx[h, p.mp] = (acc_kv[h] * factor_t[0:64, :]).astype(BF16)

        def kv_copy(i, dev):
            view = kvx.at[h, p.mp]
            return rcopy(view, view, skv.at[h, i], rkv.at[h, p.mp], dev)

        kv_to = [kv_copy(0, p.X), kv_copy(1, p.XC), kv_copy(2, p.C)]
        for cp in kv_to:
            cp.start()
        for hh in range(2):
            cols = slice(hh * 128, (hh + 1) * 128)
            q = acc_q[h, :, cols] * factor
            turned = q * cos_ref[rows_h, :] + pltpu.roll(q, 64, 1) * sin_ref[rows_h, :]
            qb[h, :, cols] = turned.astype(BF16)
        yield 2.5
        for m in (p.xo * 2 + p.c, p.xo * 2 + p.co, p.x * 2 + p.co):
            view = kvx.at[h, m]
            rcopy(view, view, skv.at[h, 0], rkv.at[h, m], p.C).wait_recv()
        state[(l, h)] = True
        assert (l, 0) in state
        keys, values = [], []
        for i in range(h + 1):
            at = slice(i * half, (i + 1) * half)
            low = jnp.concatenate([kvx[i, 0, 0:32, :], kvx[i, 1, 0:32, :]], axis=0).astype(F32)
            high = jnp.concatenate([kvx[i, 2, 0:32, :], kvx[i, 3, 0:32, :]], axis=0).astype(F32)
            cos_t, sin_t = cos_t_ref[:, at], sin_t_ref[:, at]
            keys.append(
                jnp.concatenate(
                    [low * cos_t - high * sin_t, high * cos_t + low * sin_t], axis=0
                ).astype(BF16)
            )
            values.append(jnp.concatenate([kvx[i, m, 32:64, :] for m in range(4)], axis=0))
        for hh in range(2):
            cols = slice(hh * 128, (hh + 1) * 128)
            scores = jnp.concatenate(
                [jnp.dot(qb[h, :, cols], k, preferred_element_type=F32) for k in keys], axis=1
            ) * (1.0 / math.sqrt(HEAD_DIM))
            scores = jnp.where(mask_ref[rows_h, 0 : (h + 1) * half] > 0.5, scores, -1e30)
            weights = jnp.exp(scores - jnp.max(scores, axis=-1, keepdims=True))
            weights = (weights / jnp.sum(weights, axis=-1, keepdims=True)).astype(BF16)
            out = jnp.zeros((half, HEAD_DIM), F32)
            for i, v in enumerate(values):
                out = out + lax.dot_general(
                    weights[:, i * half : (i + 1) * half],
                    v,
                    (((1,), (1,)), ((), ())),
                    preferred_element_type=F32,
                )
            attb[h, p.c, :, cols] = out.astype(BF16)
        view = attb.at[h, p.c]
        at_to = rcopy(view, view, sat.at[h], rat.at[h], p.C)
        at_to.start()
        yield 1.0
        if h == 0:
            for j in range(8):
                own_o(l, j).wait()
                give_o(l, j).wait_recv()
        view = attb.at[h, p.co]
        rcopy(view, view, sat.at[h], rat.at[h], p.C).wait_recv()

        def piece(y, x, part):
            j = y * 2 + x
            at = slice(None) if part is None else halves[part][0]
            out = jnp.dot(
                attb[h, 0, at, :], wv[l, j, 0:256, :], preferred_element_type=F32
            ) + jnp.dot(attb[h, 1, at, :], wv[l, j, 256:512, :], preferred_element_type=F32)
            return out if part is not None else [out[r, :] for r, _ in halves]

        gain = gains[min(l + 1, layers - 1), :, block(p.me)]

        def finish(part, total):
            at = slice(h * half + halves[part][0].start, h * half + halves[part][0].stop)
            new = out_ref[at, :] + total
            out_ref[at, :] = new
            if l + 1 < layers:
                gath[h, p.me, halves[part][0], :] = (new * gain).astype(BF16)

        rs = Scatter(p, sb.at[h], rb.at[h], halves, sls.at[h], rls.at[h], piece)
        yield from rs.steps(finish)
        for cp in kv_to:
            cp.wait_send()
        at_to.wait_send()

    def layer_stream(h):
        for l in range(layers):
            if l > 0:
                if h == 0:
                    for cp in loads(l):
                        cp.wait()
                yield from gather_rows(l, h)
            yield from attention(l, h)

    def weights():
        yield 0.1
        for l in range(layers):
            if l > 0:
                for cp in loads(l):
                    cp.start()
            for j in range(8):
                own_o(l, j).start()
                give_o(l, j).start()
            yield 8.0

    interleave((0.0, forward()), (0.1, text(0)), (6.0, text(1)), (4.0, weights()))
    interleave((0.0, layer_stream(0)), (3.0, layer_stream(1)), (4.0, backward()))
    for l in range(layers):
        for j in range(8):
            give_o(l, j).wait_send()


def step_call(count, small, seg, gain, patches, grads, w_in, w_out, text, q_w, kv_w, o_w):
    n_dp = 8
    xw, gw, hid = w_in.shape[0], w_out.shape[1], w_in.shape[1]
    ww = ((xw // 2 + 127) // 128) * 128
    half_out = gw // 2
    tokens, share = text.shape
    half = tokens // 2
    layers = q_w.shape[0]
    dma = pltpu.SemaphoreType.DMA
    vm = pl.BlockSpec(memory_space=pltpu.VMEM)
    hbm = pl.BlockSpec(memory_space=pl.ANY)
    V = pltpu.VMEM
    scratch = [
        V(patches.shape, BF16),
        V(grads.shape, BF16),
        V(w_in.shape, BF16),
        V(w_out.shape, BF16),
        V(text.shape, BF16),
        dma((5,)),
        V((PAD, patches.shape[1]), BF16),
        V((PAD, grads.shape[1]), BF16),
        V((n_dp, PAD, xw), BF16),
        V((n_dp, PAD, gw), BF16),
        V((2, n_dp, PAD, hid), BF16),
        V((2, n_dp, PAD, hid), BF16),
        V((2, n_dp, PAD, hid), BF16),
        V((PAD, hid), F32),
        V((n_dp, PAD, half_out), BF16),
        V((n_dp, PAD, half_out), BF16),
        V((n_dp, PAD, half_out), F32),
        V((7, PAD, half_out), BF16),
        V((7, PAD, half_out), BF16),
        V((n_dp, PAD, ww), BF16),
        V((n_dp, PAD, ww), BF16),
        V((n_dp, PAD, ww), F32),
        V((7, PAD, ww), BF16),
        V((7, PAD, ww), BF16),
        V((PAD, half_out), BF16),
        V((PAD, half_out), BF16),
        V((PAD, ww), BF16),
        V((PAD, ww), BF16),
        V((16, PAD, ww), BF16),
        V((16, PAD, share), BF16),
        V((2, 16, half, share), BF16),
        V(q_w.shape, BF16),
        V(kv_w.shape, BF16),
        V((layers, 8, 512, share), BF16),
        V((layers, 1, D), F32),
        V((layers, 1, D), F32),
        V((tokens, tokens), F32),
        V((tokens, 128), F32),
        V((tokens, 128), F32),
        V((64, tokens), F32),
        V((64, tokens), F32),
        V((2, half, 256), F32),
        V((2, 64, half), F32),
        V((2, half, 128), F32),
        V((PAD, 256), F32),
        V((64, PAD), F32),
        V((PAD, 128), F32),
        V((2, half, 256), BF16),
        V((2, 4, 64, half), BF16),
        V((2, 2, half, 256), BF16),
        V((2, 7, half, share), BF16),
        V((2, 7, half, share), BF16),
        dma((2, n_dp)),
        dma((2, n_dp)),
        dma((2, n_dp)),
        dma((2, n_dp)),
        dma((2, n_dp)),
        dma((2, n_dp)),
        dma((2, n_dp)),
        dma((2,)),
        dma((2,)),
        dma((2, 14)),
        dma((2, 14)),
        dma((2,)),
        dma((2,)),
        dma((GATHER_SENDS,)),
        dma((32,)),
        dma((GATHER_SENDS,)),
        dma((32,)),
        dma((layers,)),
        dma((layers, 2)),
        dma((layers, 8)),
        dma((layers, 8)),
        dma((layers, 8)),
        dma((2, GATHER_SENDS)),
        dma((2, 32)),
        dma((2, 3)),
        dma((2, 4)),
        dma((2,)),
        dma((2,)),
        dma((2, 14)),
        dma((2, 14)),
    ]
    return pl.pallas_call(
        step_kernel,
        out_shape=(
            jax.ShapeDtypeStruct(text.shape, F32),
            jax.ShapeDtypeStruct(patches.shape, F32),
        ),
        in_specs=[pl.BlockSpec(memory_space=pltpu.SMEM)] + [vm] * 3 + [hbm] * 8,
        out_specs=(vm, vm),
        scratch_shapes=scratch,
        compiler_params=pltpu.CompilerParams(
            collective_id=0, has_side_effects=True, vmem_limit_bytes=58 * 2**20
        ),
    )(count, small, seg, gain, patches, grads, w_in, w_out, text, q_w, kv_w, o_w)


def local(
    patches,
    ln_gain,
    ln_shift,
    w_in,
    b_in,
    w_out,
    b_out,
    place,
    image_counts,
    text_rows,
    segments,
    norm_gain,
    q_weight,
    kv_weight,
    o_weight,
    grad_rows,
):
    spots = jnp.pad(place.astype(F32), (0, 128 - place.shape[0]))
    small = jnp.concatenate(
        [x.astype(F32) for x in (ln_gain, ln_shift, b_out)] + [spots, b_in.astype(F32)]
    )[None]
    return step_call(
        image_counts,
        small,
        segments,
        norm_gain,
        patches,
        grad_rows,
        w_in,
        w_out,
        text_rows,
        q_weight,
        kv_weight,
        o_weight,
    )


def solution(mesh):
    in_specs = (
        P("dp", None),
        P(),
        P(),
        P("dp", ("sec", "mp")),
        P(("sec", "mp")),
        P(("sec", "mp"), "dp"),
        P(("sec", "mp")),
        P("dp"),
        P("dp"),
        P("dp", ("sec", "mp")),
        P("dp", None),
        P(),
        P(None, None, ("sec", "mp")),
        P(None, None, ("sec", "mp"), None),
        P(None, ("sec", "mp"), None),
        P("dp", None),
    )
    out_specs = (P("dp", ("sec", "mp")), P("dp", None))
    return jax.shard_map(local, mesh=mesh, in_specs=in_specs, out_specs=out_specs, check_vma=False)
```

time: 709 us -> 164 us (0.23)
  waiting for transfers between devices: 538 us -> 0 us
  Pallas kernels: 0 us -> 151 us
  blocking collectives: 66.9 us -> 0 us
  matrix products: 52.9 us -> 0 us
  local copies, waits for them, and re-layouts: 24.3 us -> 6.55 us
  between operations: 15.3 us -> 1.29 us
    reduce_scatter x3 -> x0, waiting for transfers between devices: 252 us -> none  [the longest x2 192 us: section_features(): lax.psum_scatter(lax.dot_general(o_local, attended, (((0,), (1,)), ((), (...]
    all_gather x4 -> x0, waiting for transfers between devices: 187 us -> none  [the longest x1 77 us: local(): lax.all_gather(w_out, 'dp', axis=1, tiled=True)]
    pallas_call x0 -> x1, Pallas kernels: none -> 151 us  [step_call(): pl.pallas_call(step_kernel, out_shape=(jax.ShapeDtypeStruct(text.shape, F...]
    psum x1 -> x0, waiting for transfers between devices: 97.3 us -> none  [merger_back(): normed_grads = lax.psum(normed_grads, ('sec', 'mp'))]
    psum x2 -> x0, blocking collectives: 55.3 us -> none  [section_features(): lax.psum(jnp.sum(rows_local * rows_local, axis=1), ('sec', 'mp'))]
    dot_general x14 -> x0, matrix products: 50.5 us -> none  [the longest x2 13.4 us: section_features(): lax.dot_general(o_local, attended, (((0,), (1,)), ((), ())), preferred_el...]
    dot_general x3 -> x0, local copies, waits for them, and re-layouts: 18.6 us -> none  [attend(): jnp.dot(normed, q_local, preferred_element_type=jnp.float32)]
    all_gather x2 -> x0, blocking collectives: 11.6 us -> none  [attend(): key_value = lax.all_gather(key_value, 'mp', axis=2, tiled=True)]
  transfers between devices with their start and end apart: 8 -> 0, of which waited for: 8 -> 0; matrix products, arithmetic and copies ran while one was open for 8% -> 0% of each run, Pallas kernels for 0% -> 0%
where the time goes in v2:
time: 164 us; the launch traced here: 162 us
  Pallas kernels  151 us (92%)
  local copies, waits for them, and re-layouts  6.55 us (4%)
  other arithmetic  3.42 us (2%)
    pallas_call x1, Pallas kernels, step_call(): pl.pallas_call(step_kernel, out_shape=(jax.ShapeDtypeStruct(text.shape, F...  151 us
    unnamed x4, local copies, waits for them, and re-layouts  5.95 us

profile of v2, /device:TPU:0, one launch (start us, length us, event | category | flops | bytes accessed | tf_op | source)
XLA Modules:
  0.0 162.2 jit_solution(9379505160357580995)
XLA Ops:
  1.3 0.7 convert_element_type.20
  1.9 0.7 convert_dynamic-update-slice_fusion.1
  2.6 0.7 convert_dynamic-update-slice_fusion
  3.3 0.7 constant_dynamic-update-slice_fusion.2
  4.0 0.7 constant_dynamic-update-slice_fusion
  4.7 0.6 broadcast_in_dim.3.small_ref
  5.3 2.0 %copy.18.w_in_hbm = bf16[640,320]{1,0:T(8,128)(2,1)} copy(bf16[640,320]{0,1:T(8,128)(2,1)} %param.19) | data formatting | bytes 819200 | tf_op args[3]
  7.3 151.0 %shard_map.167 = (f32[256,512]{1,0:T(8,128)}, f32[40,5120]{1,0:T(8,128)}) custom-call(s32[1]{0:T(128)S(6)} %copy.26.count_ref, f32[1,3520]{1,0:T(1,128)} %broadcast_in_dim.3.small_ref, s32[1,256]{1,0:T(1,128)} %seg_ref.1, bf16[2,8192]{1,0:T(2,128)(2,1)} %gain_ref.1, bf16[40,5120]{1,0:T(8,128)(2,1)} %patches_hbm.1, bf16[40,8192]{1,0:T(8,128)(2,1)} %grads_hbm.1, ...), custom_call_target="tpu_custom_call" | custom-call | tf_op jit(solution)/shard_map/pallas_call | solution.py:920
  158.3 1.9 %copy.27 = f32[256,512]{1,0:T(8,128)} copy(f32[256,512]{1,0:T(8,128)} %get-tuple-element.4) | data formatting | bytes 1048576
  160.1 2.1 %copy.28 = f32[40,5120]{1,0:T(8,128)} copy(f32[40,5120]{1,0:T(8,128)} %get-tuple-element.5) | data formatting | bytes 1638400
  (2 shorter events, 0.0 us)
